TPU v7x, 32 devices: a whole 2x2x4 slice. The times are simulated.
32 devices in a mesh: segment: 2 (over core), gx: 2 (over x), gy: 4 (over z), gz: 2 (over y).
Axes of the slice: x: 2, y: 2, z: 4, core: 2. Of those that a mesh axis runs over, the one named last changes fastest.
Arguments:
- features: bfloat16 [2, 16, 8, 128, 256], P(None, None, 'gx', 'gy', 'gz'), may hold values from -6 to 6
- weights: bfloat16 [2, 2, 16, 16, 3, 3, 3], P('segment'), may hold values from -0.4375 to 0.4375
- biases: bfloat16 [2, 2, 16], P('segment'), may hold values from -3 to 3
Outputs:
- section_out: bfloat16 [2, 2, 16, 8, 128, 256], P('segment', None, None, 'gx', 'gy', 'gz')
All inputs are finite; a program needn't handle non-finite values.
Results may differ from a plain program's by a relative error of at most 0.0054.
Values may be sent and summed in bfloat16 or wider, within the bound.
No kernel may reach another device: no remote copies, remote signals or barrier semaphores. Data moves between devices by JAX's collectives and lax.ppermute only.
A program may use at most 64 MiB of HBM per device.

v0:
```python
import jax
import jax.numpy as jnp
from jax import lax
from jax.sharding import PartitionSpec as P


def with_halo(value, sides, width):
    for axis, dim in sides:
        size, length = (lax.axis_size(axis), value.shape[dim])
        up = [(i, (i + 1) % size) for i in range(size - 1)]
        down = [(j, i) for i, j in up]
        last = lax.slice_in_dim(value, length - width, length, axis=dim)
        initial = lax.slice_in_dim(value, 0, width, axis=dim)
        before = lax.ppermute(last, axis, up)
        after = lax.ppermute(initial, axis, down)
        value = jnp.concatenate([before, value, after], axis=dim)
    return value


def band_table(width):
    source = lax.broadcasted_iota(jnp.int32, (width + 2, 3, width), 0)
    offsets = lax.broadcasted_iota(jnp.int32, (width + 2, 3, width), 1)
    target = lax.broadcasted_iota(jnp.int32, (width + 2, 3, width), 2)
    return jnp.where(source == target + offsets, 1.0, 0.0).astype(jnp.bfloat16)


def convolve(field, kernel, offset):
    padded = with_halo(field, (("gx", 1), ("gy", 2), ("gz", 3)), 1)
    depth = field.shape[1]
    height = field.shape[2]
    width = field.shape[3]
    shifted = jnp.einsum(
        "cxyw,wdz->dcxyz", padded, band_table(width), preferred_element_type=jnp.float32
    ).astype(jnp.bfloat16)
    linear = jnp.zeros((kernel.shape[0], depth, height, width), jnp.float32)
    for step_x in range(3):
        for step_y in range(3):
            slab = shifted[:, :, step_x : step_x + depth, step_y : step_y + height, :]
            taps = kernel[:, :, step_x, step_y, :]
            linear = linear + jnp.einsum(
                "oid,dixyz->oxyz", taps, slab, preferred_element_type=jnp.float32
            )
    summed = linear + offset.astype(jnp.float32)[:, None, None, None]
    return jnp.where(summed > 0, summed, 0.2 * summed).astype(jnp.bfloat16)


def section_pass(field, kernels, offsets):
    return convolve(convolve(field, kernels[0], offsets[0]), kernels[1], offsets[1])


def shards(features, weights, biases):
    section = lax.axis_index("segment")
    micro_count = features.shape[0]
    all_kernels, all_offsets = (
        lax.all_gather(weights, "segment", axis=0, tiled=True),
        lax.all_gather(biases, "segment", axis=0, tiled=True),
    )
    half_count = micro_count // 2
    my_batches = lax.dynamic_slice_in_dim(features, section * half_count, half_count, 0)
    hidden = section_pass(my_batches[0], all_kernels[0], all_offsets[0])
    first_list = [hidden]
    hidden = section_pass(hidden, all_kernels[1], all_offsets[1])
    second_list = [hidden]
    stacked = jnp.stack([jnp.stack(first_list), jnp.stack(second_list)])
    return lax.all_to_all(stacked, "segment", split_axis=0, concat_axis=1, tiled=True)


def solution(mesh):
    placed = (
        P(None, None, "gx", "gy", "gz"),
        P("segment", None, None, None, None, None, None),
        P("segment", None, None),
    )
    return jax.shard_map(
        shards,
        mesh=mesh,
        in_specs=placed,
        out_specs=P("segment", None, None, "gx", "gy", "gz"),
        check_vma=False,
    )
```

profile of v0, /device:TPU:0, one launch (start us, length us, event | category | flops | bytes accessed | tf_op | source)
XLA Modules:
  0.0 191.6 jit_solution(2719549731387878683)
XLA Ops:
  1.3 4.9 %collective-permute-start = (bf16[16,1,32,128]{3,2,1,0:T(8,128)(2,1)S(1)}, bf16[16,1,32,128]{3,2,1,0:T(8,128)(2,1)S(1)}, u32[]{:S(2)}, u32[]{:S(2)}) collective-permute-start(bf16[16,1,32,128]{3,2,1,0:T(8,128)(2,1)S(1)} %get-tuple-element.63), channel_id=1, source_target_pairs={{0,8},{1,9},{2,10},{3,11},{4,12},{5,13},{6,14},{7,15},{16,24},{17,... | collective-permute-start | bytes 393224 | tf_op jit(solution)/shard_map/ppermute | solution.py:14
  7.5 2.1 %all_gather.6 = bf16[2,2,16,16,3,3,3]{3,2,6,5,4,1,0:T(8,128)(2,1)S(1)} all-gather(bf16[1,2,16,16,3,3,3]{3,2,6,5,4,1,0:T(8,128)(2,1)S(1)} %copy-done.2), channel_id=1, replica_groups=mesh['segment'=2,'gx'=2,'gy'=4,'gz'=2] {'segment'}, dimensions={0}, use_global_device_ids=true | all-gather | bytes 82944 | tf_op jit(solution)/shard_map/all_gather | solution.py:55
  9.6 3.4 %collective-permute-done.1 = bf16[16,1,32,128]{3,2,1,0:T(8,128)(2,1)S(1)} collective-permute-done((bf16[16,1,32,128]{3,2,1,0:T(8,128)(2,1)S(1)}, bf16[16,1,32,128]{3,2,1,0:T(8,128)(2,1)S(1)}, u32[]{:S(2)}, u32[]{:S(2)}) %collective-permute-start.1) | collective-permute-done | bytes 131104 | tf_op jit(solution)/shard_map/ppermute | solution.py:15
  13.1 3.5 %collective-permute-start.2 = (bf16[16,6,1,128]{3,2,1,0:T(2,128)(2,1)S(1)}, bf16[16,6,1,128]{3,2,1,0:T(2,128)(2,1)S(1)}, u32[]{:S(2)}, u32[]{:S(2)}) collective-permute-start(bf16[16,6,1,128]{3,2,1,0:T(2,128)(2,1)S(1)} %get-tuple-element.55), channel_id=1, source_target_pairs={{0,2},{2,4},{4,6},{1,3},{3,5},{5,7},{8,10},{10,12},{12,14},{9,11},... | collective-permute-start | bytes 73736 | tf_op jit(solution)/shard_map/ppermute | solution.py:14
  18.0 1.8 all_gather.7
  19.8 2.8 %collective-permute-done.3 = bf16[16,6,1,128]{3,2,1,0:T(2,128)(2,1)S(1)} collective-permute-done((bf16[16,6,1,128]{3,2,1,0:T(2,128)(2,1)S(1)}, bf16[16,6,1,128]{3,2,1,0:T(2,128)(2,1)S(1)}, u32[]{:S(2)}, u32[]{:S(2)}) %collective-permute-start.3) | collective-permute-done | bytes 24608 | tf_op jit(solution)/shard_map/ppermute | solution.py:15
  26.2 4.5 %collective-permute-start.4 = (bf16[16,6,34,1]{2,0,3,1:T(8,128)(2,1)S(1)}, bf16[16,6,34,1]{2,0,3,1:T(8,128)(2,1)S(1)}, u32[]{:S(2)}, u32[]{:S(2)}) collective-permute-start(bf16[16,6,34,1]{2,0,3,1:T(8,128)(2,1)S(1)} %copy.44), channel_id=1, source_target_pairs={{0,1},{2,3},{4,5},{6,7},{8,9},{10,11},{12,13},{14,15},{16,17},{18,... | collective-permute-start | bytes 19592 | tf_op jit(solution)/shard_map/ppermute | solution.py:14
  33.8 2.9 %convert_bitcast_fusion.3 = bf16[3,16,6,34,128]{4,3,2,1,0:T(8,128)(2,1)S(1)} fusion(bf16[16,6,34,1]{3,2,1,0:T(8,128)(2,1)S(1)} %copy.47, bf16[16,6,1,128]{3,2,1,0:T(2,128)(2,1)S(1)} %collective-permute-done.3, bf16[16,1,32,128]{3,2,1,0:T(8,128)(2,1)S(1)} %collective-permute-done.1, bf16[16,4,32,128]{3,2,1,0:T(8,128)(2,1)S(1)} %dynamic-slice_bitcast_fusion, ...), kind=kOutput, calls=%fused_computation.7 | convolution fusion | flops 333271296 | bytes 3355392 | tf_op jit(solution)/shard_map/cxyw,wdz->dcxyz/dot_general | solution.py:32
  36.7 3.7 %fusion.370 = (bf16[3,16,4,32,128]{4,3,2,1,0:T(8,128)(2,1)S(1)}, bf16[3,16,4,32,128]{4,3,2,1,0:T(8,128)(2,1)S(1)}, bf16[3,16,4,32,128]{4,3,2,1,0:T(8,128)(2,1)S(...) fusion(bf16[3,16,6,34,128]{4,3,2,1,0:T(8,128)(2,1)S(1)} %conver, ...), kind=kLoop, calls=%fused_computation.272 | loop fusion | bytes 28311552 | tf_op jit(solution)/shard_map/slice | solution.py:38
  54.1 4.4 %collective-permute-done.7 = bf16[16,1,32,128]{3,0,2,1:T(8,128)(2,1)S(1)} collective-permute-done((bf16[16,1,32,128]{3,0,2,1:T(8,128)(2,1)S(1)}, bf16[16,1,32,128]{3,0,2,1:T(8,128)(2,1)S(1)}, u32[]{:S(2)}, u32[]{:S(2)}) %collective-permute-start.7) | collective-permute-done | bytes 131104 | tf_op jit(solution)/shard_map/ppermute | solution.py:15
  58.4 3.5 %collective-permute-start.8 = (bf16[16,6,1,128]{3,0,2,1:T(8,128)(2,1)S(1)}, bf16[16,6,1,128]{3,0,2,1:T(8,128)(2,1)S(1)}, u32[]{:S(2)}, u32[]{:S(2)}) collective-permute-start(bf16[16,6,1,128]{3,0,2,1:T(8,128)(2,1)S(1)} %get-tuple-element.53), channel_id=1, source_target_pairs={{0,2},{2,4},{4,6},{1,3},{3,5},{5,7},{8,10},{10,12},{12,14},{9,11},... | collective-permute-start | bytes 73736 | tf_op jit(solution)/shard_map/ppermute | solution.py:14
  61.9 1.5 collective-permute-start.9
  63.5 4.2 %collective-permute-done.9 = bf16[16,6,1,128]{3,0,2,1:T(8,128)(2,1)S(1)} collective-permute-done((bf16[16,6,1,128]{3,0,2,1:T(8,128)(2,1)S(1)}, bf16[16,6,1,128]{3,0,2,1:T(8,128)(2,1)S(1)}, u32[]{:S(2)}, u32[]{:S(2)}) %collective-permute-start.9) | collective-permute-done | bytes 24608 | tf_op jit(solution)/shard_map/ppermute | solution.py:15
  69.1 4.2 %collective-permute-start.10 = (bf16[16,6,34,1]{2,0,3,1:T(8,128)(2,1)S(1)}, bf16[16,6,34,1]{2,0,3,1:T(8,128)(2,1)S(1)}, u32[]{:S(2)}, u32[]{:S(2)}) collective-permute-start(bf16[16,6,34,1]{2,0,3,1:T(8,128)(2,1)S(1)} %copy.57), channel_id=1, source_target_pairs={{0,1},{2,3},{4,5},{6,7},{8,9},{10,11},{12,13},{14,15},{16,17},{18,... | collective-permute-start | bytes 19592 | tf_op jit(solution)/shard_map/ppermute | solution.py:14
  76.3 3.6 %collective-permute-done.11 = bf16[16,6,34,1]{2,0,3,1:T(8,128)(2,1)S(1)} collective-permute-done((bf16[16,6,34,1]{2,0,3,1:T(8,128)(2,1)S(1)}, bf16[16,6,34,1]{2,0,3,1:T(8,128)(2,1)S(1)}, u32[]{:S(2)}, u32[]{:S(2)}) %collective-permute-start.11) | collective-permute-done | bytes 6560 | tf_op jit(solution)/shard_map/ppermute | solution.py:15
  80.7 1.9 pad_maximum_fusion
  84.0 4.1 %fusion.369 = (bf16[3,16,4,32,128]{4,3,2,1,0:T(8,128)(2,1)S(1)}, bf16[3,16,4,32,128]{4,3,2,1,0:T(8,128)(2,1)S(1)}, bf16[3,16,4,32,128]{4,3,2,1,0:T(8,128)(2,1)S(...) fusion(bf16[3,16,6,34,128]{4,3,2,1,0:T(8,128)(2,1)S(1)} %conver, ...), kind=kLoop, calls=%fused_computation.271 | loop fusion | bytes 28311552 | tf_op jit(solution)/shard_map/slice | solution.py:38
  101.7 4.4 %collective-permute-done.13 = bf16[16,1,32,128]{3,0,2,1:T(8,128)(2,1)S(1)} collective-permute-done((bf16[16,1,32,128]{3,0,2,1:T(8,128)(2,1)S(1)}, bf16[16,1,32,128]{3,0,2,1:T(8,128)(2,1)S(1)}, u32[]{:S(2)}, u32[]{:S(2)}) %collective-permute-start.13) | collective-permute-done | bytes 131104 | tf_op jit(solution)/shard_map/ppermute | solution.py:15
  106.1 3.5 %collective-permute-start.14 = (bf16[16,6,1,128]{3,0,2,1:T(8,128)(2,1)S(1)}, bf16[16,6,1,128]{3,0,2,1:T(8,128)(2,1)S(1)}, u32[]{:S(2)}, u32[]{:S(2)}) collective-permute-start(bf16[16,6,1,128]{3,0,2,1:T(8,128)(2,1)S(1)} %get-tuple-element.51), channel_id=1, source_target_pairs={{0,2},{2,4},{4,6},{1,3},{3,5},{5,7},{8,10},{10,12},{12,14},{9,11},... | collective-permute-start | bytes 73736 | tf_op jit(solution)/shard_map/ppermute | solution.py:14
  111.1 4.2 %collective-permute-done.15 = bf16[16,6,1,128]{3,0,2,1:T(8,128)(2,1)S(1)} collective-permute-done((bf16[16,6,1,128]{3,0,2,1:T(8,128)(2,1)S(1)}, bf16[16,6,1,128]{3,0,2,1:T(8,128)(2,1)S(1)}, u32[]{:S(2)}, u32[]{:S(2)}) %collective-permute-start.15) | collective-permute-done | bytes 24608 | tf_op jit(solution)/shard_map/ppermute | solution.py:15
  116.7 1.6 collective-permute-start.16
  121.5 3.4 %collective-permute-done.17 = bf16[16,6,34,1]{2,0,3,1:T(8,128)(2,1)S(1)} collective-permute-done((bf16[16,6,34,1]{2,0,3,1:T(8,128)(2,1)S(1)}, bf16[16,6,34,1]{2,0,3,1:T(8,128)(2,1)S(1)}, u32[]{:S(2)}, u32[]{:S(2)}) %collective-permute-start.17) | collective-permute-done | bytes 6560 | tf_op jit(solution)/shard_map/ppermute | solution.py:15
  125.8 1.9 pad_maximum_fusion.1
  129.0 3.7 %fusion.368 = (bf16[3,16,4,32,128]{4,3,2,1,0:T(8,128)(2,1)S(1)}, bf16[3,16,4,32,128]{4,3,2,1,0:T(8,128)(2,1)S(1)}, bf16[3,16,4,32,128]{4,3,2,1,0:T(8,128)(2,1)S(...) fusion(bf16[3,16,6,34,128]{4,3,2,1,0:T(8,128)(2,1)S(1)} %conver, ...), kind=kLoop, calls=%fused_computation.270 | loop fusion | bytes 28311552 | tf_op jit(solution)/shard_map/slice | solution.py:38
  146.3 4.4 %collective-permute-done.19 = bf16[16,1,32,128]{3,0,2,1:T(8,128)(2,1)S(1)} collective-permute-done((bf16[16,1,32,128]{3,0,2,1:T(8,128)(2,1)S(1)}, bf16[16,1,32,128]{3,0,2,1:T(8,128)(2,1)S(1)}, u32[]{:S(2)}, u32[]{:S(2)}) %collective-permute-start.19) | collective-permute-done | bytes 131104 | tf_op jit(solution)/shard_map/ppermute | solution.py:15
  150.7 1.9 %collective-permute-start.20 = (bf16[16,6,1,128]{3,0,2,1:T(8,128)(2,1)S(1)}, bf16[16,6,1,128]{3,0,2,1:T(8,128)(2,1)S(1)}, u32[]{:S(2)}, u32[]{:S(2)}) collective-permute-start(bf16[16,6,1,128]{3,0,2,1:T(8,128)(2,1)S(1)} %get-tuple-element.49), channel_id=1, source_target_pairs={{0,2},{2,4},{4,6},{1,3},{3,5},{5,7},{8,10},{10,12},{12,14},{9,11},... | collective-permute-start | bytes 73736 | tf_op jit(solution)/shard_map/ppermute | solution.py:14
  154.1 4.2 %collective-permute-done.21 = bf16[16,6,1,128]{3,0,2,1:T(8,128)(2,1)S(1)} collective-permute-done((bf16[16,6,1,128]{3,0,2,1:T(8,128)(2,1)S(1)}, bf16[16,6,1,128]{3,0,2,1:T(8,128)(2,1)S(1)}, u32[]{:S(2)}, u32[]{:S(2)}) %collective-permute-start.21) | collective-permute-done | bytes 24608 | tf_op jit(solution)/shard_map/ppermute | solution.py:15
  159.8 1.6 collective-permute-start.22
  164.6 3.4 %collective-permute-done.23 = bf16[16,6,34,1]{2,0,3,1:T(8,128)(2,1)S(1)} collective-permute-done((bf16[16,6,34,1]{2,0,3,1:T(8,128)(2,1)S(1)}, bf16[16,6,34,1]{2,0,3,1:T(8,128)(2,1)S(1)}, u32[]{:S(2)}, u32[]{:S(2)}) %collective-permute-start.23) | collective-permute-done | bytes 6560 | tf_op jit(solution)/shard_map/ppermute | solution.py:15
  168.8 1.9 pad_maximum_fusion.2
  172.1 3.7 %fusion.367 = (bf16[3,16,4,32,128]{4,3,2,1,0:T(8,128)(2,1)S(1)}, bf16[3,16,4,32,128]{4,3,2,1,0:T(8,128)(2,1)S(1)}, bf16[3,16,4,32,128]{4,3,2,1,0:T(8,128)(2,1)S(...) fusion(bf16[3,16,6,34,128]{4,3,2,1,0:T(8,128)(2,1)S(1)} %conver, ...), kind=kLoop, calls=%fused_computation.269 | loop fusion | bytes 28311552 | tf_op jit(solution)/shard_map/slice | solution.py:38
  185.4 4.7 %all_to_all.12 = bf16[2,1,16,4,32,128]{5,2,4,3,1,0:T(8,128)(2,1)S(1)} all-to-all(bf16[2,1,16,4,32,128]{5,2,4,3,1,0:T(8,128)(2,1)S(1)} %pad_maximum_fusion.3), channel_id=1, replica_groups=mesh['segment'=2,'gx'=2,'gy'=4,'gz'=2] {'segment'}, dimensions={0} | all-to-all | bytes 2097152 | tf_op jit(solution)/shard_map/all_to_all | solution.py:65
  (111 shorter events, 85.5 us)
Async XLA Ops:
  0.0 1.2 copy-start
  0.0 7.5 %copy-start.2 = (bf16[1,2,16,16,3,3,3]{3,2,6,5,4,1,0:T(8,128)(2,1)S(1)}, bf16[1,2,16,16,3,3,3]{3,2,6,5,4,1,0:T(8,128)(2,1)}, u32[]{:S(2)}) copy-start(bf16[1,2,16,16,3,3,3]{3,2,6,5,4,1,0:T(8,128)(2,1)} %param.4) | copy-start | bytes 82948
  1.3 16.7 %copy-start.3 = (bf16[1,2,16]{2,1,0:T(2,128)(2,1)S(1)}, bf16[1,2,16]{2,1,0:T(2,128)(2,1)}, u32[]{:S(2)}) copy-start(bf16[1,2,16]{2,1,0:T(2,128)(2,1)} %param.5) | copy-start | bytes 196
  1.3 8.3 %collective-permute-start = (bf16[16,1,32,128]{3,2,1,0:T(8,128)(2,1)S(1)}, bf16[16,1,32,128]{3,2,1,0:T(8,128)(2,1)S(1)}, u32[]{:S(2)}, u32[]{:S(2)}) collective-permute-start(bf16[16,1,32,128]{3,2,1,0:T(8,128)(2,1)S(1)} %get-tuple-element.63), channel_id=1, source_target_pairs={{0,8},{1,9},{2,10},{3,11},{4,12},{5,13},{6,14},{7,15},{16,24},{17,... | collective-permute-start | bytes 393224 | tf_op jit(solution)/shard_map/ppermute | solution.py:14
  6.2 6.9 %collective-permute-start.1 = (bf16[16,1,32,128]{3,2,1,0:T(8,128)(2,1)S(1)}, bf16[16,1,32,128]{3,2,1,0:T(8,128)(2,1)S(1)}, u32[]{:S(2)}, u32[]{:S(2)}) collective-permute-start(bf16[16,1,32,128]{3,2,1,0:T(8,128)(2,1)S(1)} %get-tuple-element.64), channel_id=1, source_target_pairs={{8,0},{9,1},{10,2},{11,3},{12,4},{13,5},{14,6},{15,7},{24,16},{25,... | collective-permute-start | bytes 393224 | tf_op jit(solution)/shard_map/ppermute | solution.py:15
  13.1 6.7 %collective-permute-start.2 = (bf16[16,6,1,128]{3,2,1,0:T(2,128)(2,1)S(1)}, bf16[16,6,1,128]{3,2,1,0:T(2,128)(2,1)S(1)}, u32[]{:S(2)}, u32[]{:S(2)}) collective-permute-start(bf16[16,6,1,128]{3,2,1,0:T(2,128)(2,1)S(1)} %get-tuple-element.55), channel_id=1, source_target_pairs={{0,2},{2,4},{4,6},{1,3},{3,5},{5,7},{8,10},{10,12},{12,14},{9,11},... | collective-permute-start | bytes 73736 | tf_op jit(solution)/shard_map/ppermute | solution.py:14
  16.6 6.0 %collective-permute-start.3 = (bf16[16,6,1,128]{3,2,1,0:T(2,128)(2,1)S(1)}, bf16[16,6,1,128]{3,2,1,0:T(2,128)(2,1)S(1)}, u32[]{:S(2)}, u32[]{:S(2)}) collective-permute-start(bf16[16,6,1,128]{3,2,1,0:T(2,128)(2,1)S(1)} %get-tuple-element.56), channel_id=1, source_target_pairs={{2,0},{4,2},{6,4},{3,1},{5,3},{7,5},{10,8},{12,10},{14,12},{11,9},... | collective-permute-start | bytes 73736 | tf_op jit(solution)/shard_map/ppermute | solution.py:15
  24.9 8.1 %collective-permute-start.5 = (bf16[16,6,34,1]{2,0,3,1:T(8,128)(2,1)S(1)}, bf16[16,6,34,1]{2,0,3,1:T(8,128)(2,1)S(1)}, u32[]{:S(2)}, u32[]{:S(2)}) collective-permute-start(bf16[16,6,34,1]{2,0,3,1:T(8,128)(2,1)S(1)} %copy.45), channel_id=1, source_target_pairs={{1,0},{3,2},{5,4},{7,6},{9,8},{11,10},{13,12},{15,14},{17,16},{19,... | collective-permute-start | bytes 19592 | tf_op jit(solution)/shard_map/ppermute | solution.py:15
  26.2 6.1 %collective-permute-start.4 = (bf16[16,6,34,1]{2,0,3,1:T(8,128)(2,1)S(1)}, bf16[16,6,34,1]{2,0,3,1:T(8,128)(2,1)S(1)}, u32[]{:S(2)}, u32[]{:S(2)}) collective-permute-start(bf16[16,6,34,1]{2,0,3,1:T(8,128)(2,1)S(1)} %copy.44), channel_id=1, source_target_pairs={{0,1},{2,3},{4,5},{6,7},{8,9},{10,11},{12,13},{14,15},{16,17},{18,... | collective-permute-start | bytes 19592 | tf_op jit(solution)/shard_map/ppermute | solution.py:14
  50.1 4.0 %collective-permute-start.6 = (bf16[16,1,32,128]{3,0,2,1:T(8,128)(2,1)S(1)}, bf16[16,1,32,128]{3,0,2,1:T(8,128)(2,1)S(1)}, u32[]{:S(2)}, u32[]{:S(2)}) collective-permute-start(bf16[16,1,32,128]{3,0,2,1:T(8,128)(2,1)S(1)} %get-tuple-element.61), channel_id=1, source_target_pairs={{0,8},{1,9},{2,10},{3,11},{4,12},{5,13},{6,14},{7,15},{16,24},{17,... | collective-permute-start | bytes 393224 | tf_op jit(solution)/shard_map/ppermute | solution.py:14
  51.6 6.9 %collective-permute-start.7 = (bf16[16,1,32,128]{3,0,2,1:T(8,128)(2,1)S(1)}, bf16[16,1,32,128]{3,0,2,1:T(8,128)(2,1)S(1)}, u32[]{:S(2)}, u32[]{:S(2)}) collective-permute-start(bf16[16,1,32,128]{3,0,2,1:T(8,128)(2,1)S(1)} %get-tuple-element.62), channel_id=1, source_target_pairs={{8,0},{9,1},{10,2},{11,3},{12,4},{13,5},{14,6},{15,7},{24,16},{25,... | collective-permute-start | bytes 393224 | tf_op jit(solution)/shard_map/ppermute | solution.py:15
  58.4 5.0 %collective-permute-start.8 = (bf16[16,6,1,128]{3,0,2,1:T(8,128)(2,1)S(1)}, bf16[16,6,1,128]{3,0,2,1:T(8,128)(2,1)S(1)}, u32[]{:S(2)}, u32[]{:S(2)}) collective-permute-start(bf16[16,6,1,128]{3,0,2,1:T(8,128)(2,1)S(1)} %get-tuple-element.53), channel_id=1, source_target_pairs={{0,2},{2,4},{4,6},{1,3},{3,5},{5,7},{8,10},{10,12},{12,14},{9,11},... | collective-permute-start | bytes 73736 | tf_op jit(solution)/shard_map/ppermute | solution.py:14
  61.9 5.7 %collective-permute-start.9 = (bf16[16,6,1,128]{3,0,2,1:T(8,128)(2,1)S(1)}, bf16[16,6,1,128]{3,0,2,1:T(8,128)(2,1)S(1)}, u32[]{:S(2)}, u32[]{:S(2)}) collective-permute-start(bf16[16,6,1,128]{3,0,2,1:T(8,128)(2,1)S(1)} %get-tuple-element.54), channel_id=1, source_target_pairs={{2,0},{4,2},{6,4},{3,1},{5,3},{7,5},{10,8},{12,10},{14,12},{11,9},... | collective-permute-start | bytes 73736 | tf_op jit(solution)/shard_map/ppermute | solution.py:15
  69.1 6.4 %collective-permute-start.10 = (bf16[16,6,34,1]{2,0,3,1:T(8,128)(2,1)S(1)}, bf16[16,6,34,1]{2,0,3,1:T(8,128)(2,1)S(1)}, u32[]{:S(2)}, u32[]{:S(2)}) collective-permute-start(bf16[16,6,34,1]{2,0,3,1:T(8,128)(2,1)S(1)} %copy.57), channel_id=1, source_target_pairs={{0,1},{2,3},{4,5},{6,7},{8,9},{10,11},{12,13},{14,15},{16,17},{18,... | collective-permute-start | bytes 19592 | tf_op jit(solution)/shard_map/ppermute | solution.py:14
  74.2 5.7 %collective-permute-start.11 = (bf16[16,6,34,1]{2,0,3,1:T(8,128)(2,1)S(1)}, bf16[16,6,34,1]{2,0,3,1:T(8,128)(2,1)S(1)}, u32[]{:S(2)}, u32[]{:S(2)}) collective-permute-start(bf16[16,6,34,1]{2,0,3,1:T(8,128)(2,1)S(1)} %copy.58), channel_id=1, source_target_pairs={{1,0},{3,2},{5,4},{7,6},{9,8},{11,10},{13,12},{15,14},{17,16},{19,... | collective-permute-start | bytes 19592 | tf_op jit(solution)/shard_map/ppermute | solution.py:15
  97.7 4.0 %collective-permute-start.12 = (bf16[16,1,32,128]{3,0,2,1:T(8,128)(2,1)S(1)}, bf16[16,1,32,128]{3,0,2,1:T(8,128)(2,1)S(1)}, u32[]{:S(2)}, u32[]{:S(2)}) collective-permute-start(bf16[16,1,32,128]{3,0,2,1:T(8,128)(2,1)S(1)} %get-tuple-element.59), channel_id=1, source_target_pairs={{0,8},{1,9},{2,10},{3,11},{4,12},{5,13},{6,14},{7,15},{16,24},{17,... | collective-permute-start | bytes 393224 | tf_op jit(solution)/shard_map/ppermute | solution.py:14
  99.2 6.9 %collective-permute-start.13 = (bf16[16,1,32,128]{3,0,2,1:T(8,128)(2,1)S(1)}, bf16[16,1,32,128]{3,0,2,1:T(8,128)(2,1)S(1)}, u32[]{:S(2)}, u32[]{:S(2)}) collective-permute-start(bf16[16,1,32,128]{3,0,2,1:T(8,128)(2,1)S(1)} %get-tuple-element.60), channel_id=1, source_target_pairs={{8,0},{9,1},{10,2},{11,3},{12,4},{13,5},{14,6},{15,7},{24,16},{25,... | collective-permute-start | bytes 393224 | tf_op jit(solution)/shard_map/ppermute | solution.py:15
  106.1 5.0 %collective-permute-start.14 = (bf16[16,6,1,128]{3,0,2,1:T(8,128)(2,1)S(1)}, bf16[16,6,1,128]{3,0,2,1:T(8,128)(2,1)S(1)}, u32[]{:S(2)}, u32[]{:S(2)}) collective-permute-start(bf16[16,6,1,128]{3,0,2,1:T(8,128)(2,1)S(1)} %get-tuple-element.51), channel_id=1, source_target_pairs={{0,2},{2,4},{4,6},{1,3},{3,5},{5,7},{8,10},{10,12},{12,14},{9,11},... | collective-permute-start | bytes 73736 | tf_op jit(solution)/shard_map/ppermute | solution.py:14
  109.6 5.7 %collective-permute-start.15 = (bf16[16,6,1,128]{3,0,2,1:T(8,128)(2,1)S(1)}, bf16[16,6,1,128]{3,0,2,1:T(8,128)(2,1)S(1)}, u32[]{:S(2)}, u32[]{:S(2)}) collective-permute-start(bf16[16,6,1,128]{3,0,2,1:T(8,128)(2,1)S(1)} %get-tuple-element.52), channel_id=1, source_target_pairs={{2,0},{4,2},{6,4},{3,1},{5,3},{7,5},{10,8},{12,10},{14,12},{11,9},... | collective-permute-start | bytes 73736 | tf_op jit(solution)/shard_map/ppermute | solution.py:15
  116.7 4.0 %collective-permute-start.16 = (bf16[16,6,34,1]{2,0,3,1:T(8,128)(2,1)S(1)}, bf16[16,6,34,1]{2,0,3,1:T(8,128)(2,1)S(1)}, u32[]{:S(2)}, u32[]{:S(2)}) collective-permute-start(bf16[16,6,34,1]{2,0,3,1:T(8,128)(2,1)S(1)} %copy.71), channel_id=1, source_target_pairs={{0,1},{2,3},{4,5},{6,7},{8,9},{10,11},{12,13},{14,15},{16,17},{18,... | collective-permute-start | bytes 19592 | tf_op jit(solution)/shard_map/ppermute | solution.py:14
  119.2 5.7 %collective-permute-start.17 = (bf16[16,6,34,1]{2,0,3,1:T(8,128)(2,1)S(1)}, bf16[16,6,34,1]{2,0,3,1:T(8,128)(2,1)S(1)}, u32[]{:S(2)}, u32[]{:S(2)}) collective-permute-start(bf16[16,6,34,1]{2,0,3,1:T(8,128)(2,1)S(1)} %copy.72), channel_id=1, source_target_pairs={{1,0},{3,2},{5,4},{7,6},{9,8},{11,10},{13,12},{15,14},{17,16},{19,... | collective-permute-start | bytes 19592 | tf_op jit(solution)/shard_map/ppermute | solution.py:15
  142.3 4.0 %collective-permute-start.18 = (bf16[16,1,32,128]{3,0,2,1:T(8,128)(2,1)S(1)}, bf16[16,1,32,128]{3,0,2,1:T(8,128)(2,1)S(1)}, u32[]{:S(2)}, u32[]{:S(2)}) collective-permute-start(bf16[16,1,32,128]{3,0,2,1:T(8,128)(2,1)S(1)} %get-tuple-element.57), channel_id=1, source_target_pairs={{0,8},{1,9},{2,10},{3,11},{4,12},{5,13},{6,14},{7,15},{16,24},{17,... | collective-permute-start | bytes 393224 | tf_op jit(solution)/shard_map/ppermute | solution.py:14
  143.8 6.9 %collective-permute-start.19 = (bf16[16,1,32,128]{3,0,2,1:T(8,128)(2,1)S(1)}, bf16[16,1,32,128]{3,0,2,1:T(8,128)(2,1)S(1)}, u32[]{:S(2)}, u32[]{:S(2)}) collective-permute-start(bf16[16,1,32,128]{3,0,2,1:T(8,128)(2,1)S(1)} %get-tuple-element.58), channel_id=1, source_target_pairs={{8,0},{9,1},{10,2},{11,3},{12,4},{13,5},{14,6},{15,7},{24,16},{25,... | collective-permute-start | bytes 393224 | tf_op jit(solution)/shard_map/ppermute | solution.py:15
  150.7 3.4 %collective-permute-start.20 = (bf16[16,6,1,128]{3,0,2,1:T(8,128)(2,1)S(1)}, bf16[16,6,1,128]{3,0,2,1:T(8,128)(2,1)S(1)}, u32[]{:S(2)}, u32[]{:S(2)}) collective-permute-start(bf16[16,6,1,128]{3,0,2,1:T(8,128)(2,1)S(1)} %get-tuple-element.49), channel_id=1, source_target_pairs={{0,2},{2,4},{4,6},{1,3},{3,5},{5,7},{8,10},{10,12},{12,14},{9,11},... | collective-permute-start | bytes 73736 | tf_op jit(solution)/shard_map/ppermute | solution.py:14
  152.6 5.7 %collective-permute-start.21 = (bf16[16,6,1,128]{3,0,2,1:T(8,128)(2,1)S(1)}, bf16[16,6,1,128]{3,0,2,1:T(8,128)(2,1)S(1)}, u32[]{:S(2)}, u32[]{:S(2)}) collective-permute-start(bf16[16,6,1,128]{3,0,2,1:T(8,128)(2,1)S(1)} %get-tuple-element.50), channel_id=1, source_target_pairs={{2,0},{4,2},{6,4},{3,1},{5,3},{7,5},{10,8},{12,10},{14,12},{11,9},... | collective-permute-start | bytes 73736 | tf_op jit(solution)/shard_map/ppermute | solution.py:15
  159.8 4.0 %collective-permute-start.22 = (bf16[16,6,34,1]{2,0,3,1:T(8,128)(2,1)S(1)}, bf16[16,6,34,1]{2,0,3,1:T(8,128)(2,1)S(1)}, u32[]{:S(2)}, u32[]{:S(2)}) collective-permute-start(bf16[16,6,34,1]{2,0,3,1:T(8,128)(2,1)S(1)} %copy.85), channel_id=1, source_target_pairs={{0,1},{2,3},{4,5},{6,7},{8,9},{10,11},{12,13},{14,15},{16,17},{18,... | collective-permute-start | bytes 19592 | tf_op jit(solution)/shard_map/ppermute | solution.py:14
  162.2 5.7 %collective-permute-start.23 = (bf16[16,6,34,1]{2,0,3,1:T(8,128)(2,1)S(1)}, bf16[16,6,34,1]{2,0,3,1:T(8,128)(2,1)S(1)}, u32[]{:S(2)}, u32[]{:S(2)}) collective-permute-start(bf16[16,6,34,1]{2,0,3,1:T(8,128)(2,1)S(1)} %copy.86), channel_id=1, source_target_pairs={{1,0},{3,2},{5,4},{7,6},{9,8},{11,10},{13,12},{15,14},{17,16},{19,... | collective-permute-start | bytes 19592 | tf_op jit(solution)/shard_map/ppermute | solution.py:15
  185.4 6.0 %copy-start.1 = (bf16[2,16,4,32,128]{4,3,2,1,0:T(8,128)(2,1)S(1)}, bf16[2,16,4,32,128]{4,3,2,1,0:T(8,128)(2,1)}, u32[]{:S(2)}) copy-start(bf16[2,16,4,32,128]{4,3,2,1,0:T(8,128)(2,1)} %param.3) | copy-start | bytes 3145732
where the time goes:
time: 195 us; the launch traced here: 192 us
  starting transfers between devices  49.8 us (26%)
  waiting for transfers between devices  47.8 us (25%)
  matrix products  45.5 us (23%)
  local copies, waits for them, and re-layouts  32.2 us (17%)
  blocking collectives  8.64 us (4%)
  other arithmetic  6.92 us (4%)
    ppermute x12, waiting for transfers between devices, with_halo(): after = lax.ppermute(initial, axis, down)  42.3 us
    dot_general x36, matrix products, convolve(): jnp.einsum('oid,dixyz->oxyz', taps, slab, preferred_element_type=jnp.floa...  38.4 us
    ppermute x12, starting transfers between devices, with_halo(): before = lax.ppermute(last, axis, up)  33.7 us
    ppermute x12, starting transfers between devices, with_halo(): after = lax.ppermute(initial, axis, down)  16.1 us
    slice x4, local copies, waits for them, and re-layouts, convolve(): slab = shifted[:, :, step_x:step_x + depth, step_y:step_y + height, :]  15 us
    dot_general x4, matrix products, convolve(): jnp.einsum('cxyw,wdz->dcxyz', padded, band_table(width), preferred_elemen...  7.04 us
    concatenate x7, other arithmetic, with_halo(): value = jnp.concatenate([before, value, after], axis=dim)  6.71 us
    ppermute x12, waiting for transfers between devices, with_halo(): before = lax.ppermute(last, axis, up)  5.5 us
  transfers between devices with their start and end apart: 24, of which 17 were waited for; matrix products, arithmetic and copies ran while one was open for 3% of the time, Pallas kernels for 0%

commit v1 on v0

v1 whole, which is shorter than its diff:
```python
import functools

import jax
import jax.numpy as jnp
from jax import lax
from jax.experimental import pallas as pl
from jax.experimental.pallas import tpu as pltpu
from jax.sharding import PartitionSpec as P

WIDE = 4
SEG = 16
BF = jnp.bfloat16
F32 = jnp.float32


def swap_pairs(size):
    return [(i, i ^ 1) for i in range(size) if i ^ 1 < size]


def shifted_pairs(size):
    return [(i, j) for i in range(1, size - 1, 2) for j in [i + 1]] + [
        (i + 1, i) for i in range(1, size - 1, 2)
    ]


def transposer():
    row = lax.broadcasted_iota(jnp.int32, (256, 256), 0)
    col = lax.broadcasted_iota(jnp.int32, (256, 256), 1)
    hit = ((row >> 4) == (col & 15)) & ((row & 15) == (col >> 4))
    return jnp.where(hit, 1.0, 0.0).astype(BF)


def lane_mask(test):
    lane = lax.broadcasted_iota(jnp.int32, (16, 128), 1)
    return jnp.where(test(lane), 1.0, 0.0).astype(BF)


def swap_rows(turn, blocks):
    wide = jnp.concatenate(blocks, 1) if len(blocks) > 1 else blocks[0]
    turned = jnp.dot(turn, wide, preferred_element_type=F32).astype(BF)
    return [turned[:, k * 128 : (k + 1) * 128].reshape(16, 16, 128) for k in range(len(blocks))]


def to_tiles(turn, ref, x, store):
    rows = ref.shape[2]
    starts = list(range(0, rows, 16))
    for k in range(0, len(starts), 2):
        some = starts[k : k + 2]
        for y0, block in zip(some, swap_rows(turn, [ref[:, x, y0 : y0 + 16, :].reshape(256, 128) for y0 in some])):
            store(y0, block)


def pack_kernel(x_ref, tile_ref, z_ref, a_ref, b_ref):
    depth, rows = tile_ref.shape[0], tile_ref.shape[1]
    right = lax.axis_index("gz") == 0
    even = lax.rem(lax.axis_index("gy"), 2) == 0
    turn = transposer()
    turned_by = jnp.where(right, WIDE, 0)
    for x in range(depth):

        def store(y0, block):
            tile_ref[x, y0 : y0 + 16] = block

        to_tiles(turn, x_ref, x, store)
    for x in range(depth):
        parts = [jnp.zeros((16, 128), BF) for _ in range(4)]
        for y in range(rows):
            mask = lane_mask(lambda lane: (lane >> 2) == y)
            moved = pltpu.roll(tile_ref[x, y], 4 * y, 1) if y else tile_ref[x, y]
            early = lane_mask(lambda lane: (((lane + turned_by) & 127) >> 2) == y)
            parts[y % 4] = parts[y % 4] + moved * early
        total = (parts[0] + parts[1]) + (parts[2] + parts[3])
        z_ref[x] = pltpu.roll(total, turned_by, 1)
    first = jnp.where(even, rows - WIDE, 0)
    second = jnp.where(even, 0, rows - WIDE)
    for x in range(depth):
        a_ref[x * WIDE : (x + 1) * WIDE] = tile_ref[x, pl.ds(first, WIDE)]
        b_ref[x * WIDE : (x + 1) * WIDE] = tile_ref[x, pl.ds(second, WIDE)]


def weight_kernel(flip_x, w_ref, b_ref, t_ref):
    layers = w_ref.shape[0]
    zero = jnp.zeros((16, 16), BF)
    flipped = lax.axis_index("gx") == 1 if flip_x else None
    row = lax.broadcasted_iota(jnp.int32, (16, 16), 0)
    col = lax.broadcasted_iota(jnp.int32, (16, 16), 1)
    for layer in range(layers):
        for dz in range(3):
            for xo in range(2):
                for yo in range(2):
                    pieces = []
                    for xi in range(4):
                        for yi in range(4):
                            dx, dy = xi - xo, yi - yo
                            if 0 <= dx < 3 and 0 <= dy < 3:
                                at = jnp.where(flipped, 2 - dx, dx) if flip_x else dx
                                pieces.append(w_ref[layer, at, dy, dz])
                            else:
                                pieces.append(zero)
                    at_row = ((dz * 2 + xo) * 2 + yo) * 16
                    t_ref[layer, at_row : at_row + 16] = jnp.concatenate(pieces, 1)
        spread = jnp.broadcast_to(b_ref[layer : layer + 1, :].astype(F32), (16, 16))
        column = jnp.sum(jnp.where(row == col, spread, 0.0), axis=1, keepdims=True)
        t_ref[layer, 192:208] = jnp.broadcast_to(column, (16, 256)).astype(BF)


def main_kernel(two_sided, counts, own_ref, halo_ref, *rest):
    sides = 2 if two_sided else 1
    raws, halos = rest[:sides], rest[sides : 2 * sides]
    t_ref, keep_ref, send_ref = rest[2 * sides : 2 * sides + 3]
    va, vb, sa, sb, bias_ref, out_ref, sems = rest[2 * sides + 3 :]
    depth, rows = own_ref.shape[0], own_ref.shape[1]
    ext_rows = rows + 2 * WIDE
    per = sa.shape[1] - 2
    segments = 128 // SEG
    blk = depth * WIDE + depth
    section = lax.axis_index("segment")
    gx, gy = lax.axis_index("gx"), lax.axis_index("gy")
    right = lax.axis_index("gz") == 0
    even = lax.rem(gy, 2) == 0
    top_ok = jnp.where(gy == 0, 0.0, 1.0).astype(F32)
    low_ok = jnp.where(gy == counts["gy"] - 1, 0.0, 1.0).astype(F32)
    prev_at = jnp.where(even, blk, 0)
    next_at = jnp.where(even, 0, blk)
    turn = transposer()
    zero_tile = jnp.zeros((16, 128), BF)

    def flip(i):
        return i if two_sided else jnp.where(gx == 1, depth - 1 - i, i)

    slabs = [(0, flip(i)) for i in range(depth)]
    if two_sided:
        slabs = [(1, depth - WIDE + i) for i in range(WIDE)] + slabs + [(2, i) for i in range(WIDE)]
        own_at = WIDE
    else:
        slabs = slabs + [(1, flip(i)) for i in range(WIDE)]
        own_at = 0
    ext = len(slabs)

    for v, s in ((va, sa), (vb, sb)):
        for x in (0, ext + 1):
            v[x] = jnp.zeros(v.shape[1:], BF)
            s[x] = jnp.zeros(s.shape[1:], BF)
        for x in range(ext + 2):
            v[x, 0] = zero_tile
            v[x, ext_rows + 1] = zero_tile

    ahead = jnp.where(right, 3 * WIDE, 0)
    own_masks = [
        lane_mask(
            lambda lane: ((((lane + ahead) & 127) >> 4) == j) & (((lane + ahead) & 15) < 3 * WIDE)
        )
        for j in range(segments)
    ]
    halo_masks = [lane_mask(lambda lane: ((lane >> 4) == j) & ((lane & 15) < WIDE)) for j in range(segments)]
    own_turn = jnp.where(right, 3 * WIDE, WIDE)
    halo_turn = jnp.where(right, 3 * WIDE, 0)

    for p, (source, i) in enumerate(slabs):
        h = halo_ref if source == 0 else halos[source - 1]
        if source == 0:
            va[p + 1, 1 + WIDE : 1 + WIDE + rows] = own_ref[i]
        else:

            def store(y0, block):
                va[p + 1, 1 + WIDE + y0 : 1 + WIDE + y0 + 16] = block

            to_tiles(turn, raws[source - 1], i, store)
        va[p + 1, 1 : 1 + WIDE] = h[pl.ds(prev_at + i * WIDE, WIDE)]
        va[p + 1, 1 + WIDE + rows : 1 + 2 * WIDE + rows] = h[pl.ds(next_at + i * WIDE, WIDE)]
        edge_prev = h[prev_at + depth * WIDE + i]
        edge_own = h[2 * blk + i]
        edge_next = h[next_at + depth * WIDE + i]
        for yo in range(per):
            own_sum, halo_sum = zero_tile, zero_tile
            for j in range(segments):
                r = per * j + yo
                if r >= ext_rows:
                    continue
                row = va[p + 1, 1 + r]
                own_sum = own_sum + (pltpu.roll(row, SEG * j, 1) if j else row) * own_masks[j]
                if r < WIDE:
                    edge, lane = edge_prev, WIDE * (rows - WIDE + r)
                elif r < WIDE + rows:
                    edge, lane = edge_own, WIDE * (r - WIDE)
                else:
                    edge, lane = edge_next, WIDE * (r - WIDE - rows)
                by = (SEG * j - lane) % 128
                halo_sum = halo_sum + (pltpu.roll(edge, by, 1) if by else edge) * halo_masks[j]
            sa[p + 1, 1 + yo] = pltpu.roll(own_sum, own_turn, 1) + pltpu.roll(halo_sum, halo_turn, 1)
        sa[p + 1, 0] = pltpu.roll(sa[p + 1, per], SEG, 1)
        sa[p + 1, per + 1] = pltpu.roll(sa[p + 1, 1], 128 - SEG, 1)

    for layer in range(4):
        one = t_ref[layer, 192:208, :128].astype(F32)
        for k in range(4):
            bias_ref[layer, 16 * k : 16 * (k + 1)] = one

    wide_lane = lax.broadcasted_iota(jnp.int32, (64, 128), 1)
    not_first = jnp.where(wide_lane == 0, 0.0, 1.0)
    not_last = jnp.where(wide_lane == 127, 0.0, 1.0)
    strip_lane = lax.broadcasted_iota(jnp.int32, (16, 128), 1) >> 4

    def strip_ok(yo):
        r = strip_lane * per + yo
        return jnp.where(r < WIDE, top_ok, jnp.where(r >= WIDE + rows, low_ok, 1.0))

    def run_layer(layer, src, dst, ssrc, sdst, x0, groups, r0, row_groups):
        last = layer == 3

        def body(g, carry):
            at = x0 + 2 * g
            items = [(src, r0 + 2 * k, False) for k in range(row_groups)]
            items += [(ssrc, 2 * k, True) for k in range(per // 2)]
            half = len(items) // 2
            order = [[items[k], items[half + k]] for k in range(half)] + [[t] for t in items[2 * half :]]
            for pair in order:
                columns = [
                    jnp.concatenate([ref[at + xi, r : r + 4].reshape(64, 128) for xi in range(4)], 0)
                    for ref, r, _ in pair
                ]
                wide = jnp.concatenate(columns, 1) if len(columns) > 1 else columns[0]
                got = jnp.dot(t_ref[layer, :192], wide, preferred_element_type=F32)
                for k, (_, r, strip) in enumerate(pair):
                    part = got[:, 128 * k : 128 * (k + 1)]
                    a = part[64:128] + pltpu.roll(part[:64], 1, 1) * not_first
                    a = a + pltpu.roll(part[128:], 127, 1) * not_last
                    a = a + bias_ref[layer]
                    a = jnp.maximum(a, 0.2 * a)
                    for xo in range(2):
                        for yo in range(2):
                            one = a[(2 * xo + yo) * 16 : (2 * xo + yo + 1) * 16]
                            if not last:
                                if strip:
                                    one = one * strip_ok(r + yo)
                                elif r + yo < WIDE:
                                    one = one * top_ok
                                elif r + yo >= WIDE + rows:
                                    one = one * low_ok
                                if two_sided:
                                    place = at + xo
                                    outside = ((place < WIDE) & (gx == 0)) | (
                                        (place >= WIDE + depth) & (gx == counts["gx"] - 1)
                                    )
                                    one = one * jnp.where(outside, 0.0, 1.0)
                            one = one.astype(BF)
                            if strip:
                                sdst[at + xo + 1, r + yo + 1] = one
                                if r + yo == 0:
                                    sdst[at + xo + 1, per + 1] = pltpu.roll(one, 128 - SEG, 1)
                                if r + yo == per - 1:
                                    sdst[at + xo + 1, 0] = pltpu.roll(one, SEG, 1)
                            else:
                                dst[at + xo + 1, r + yo + 1] = one
            return carry

        lax.fori_loop(0, groups, body, 0)

    edge_turn = jnp.where(right, 0, 2 * WIDE)
    edge_ahead = jnp.where(right, WIDE, 0)
    edge_mask = lane_mask(lambda lane: ((lane + edge_ahead) & 127) < WIDE)
    inner_mask = lane_mask(lambda lane: ((lane + edge_ahead) & 127) >= WIDE)

    def copies(part):
        return (
            pltpu.make_async_copy(out_ref.at[part], keep_ref.at[section], sems.at[part]),
            pltpu.make_async_copy(out_ref.at[part], send_ref, sems.at[part]),
        )

    def emit(part, v, s):
        for i in range(depth):
            p = own_at + i
            to = flip(i)
            starts = list(range(0, rows, 16))
            for k in range(0, len(starts), 2):
                some = starts[k : k + 2]
                blocks = []
                for y0 in some:
                    tiles = []
                    for y in range(y0, y0 + 16):
                        r = y + WIDE
                        j, yo = r // per, r % per
                        by = (128 - 3 * WIDE - SEG * j) % 128
                        edge = pltpu.roll(s[p + 1, yo + 1], by + edge_turn, 1)
                        tiles.append(v[p + 1, r + 1] * inner_mask + edge * edge_mask)
                    blocks.append(jnp.concatenate(tiles, 0))
                for y0, block in zip(some, swap_rows(turn, blocks)):
                    out_ref[part, :, to, y0 : y0 + 16] = block
        keep, send = copies(part)

        @pl.when(section == part)
        def _():
            keep.start()

        @pl.when(section != part)
        def _():
            send.start()

    half_rows = ext_rows // 2
    spans = []
    for layer in range(1, 5):
        if two_sided:
            spans.append((layer, (ext - 2 * layer) // 2))
        else:
            spans.append((0, (depth + WIDE - layer + 1) // 2))
    run_layer(0, va, vb, sa, sb, *spans[0], 0, half_rows)
    run_layer(1, vb, va, sb, sa, *spans[1], 2, half_rows - 2)
    emit(0, va, sa)
    run_layer(2, va, vb, sa, sb, *spans[2], 2, half_rows - 2)
    run_layer(3, vb, va, sb, sa, *spans[3], WIDE, rows // 2)
    emit(1, va, sa)
    for part in range(2):
        keep, send = copies(part)

        @pl.when(section == part)
        def _():
            keep.wait()

        @pl.when(section != part)
        def _():
            send.wait()


VMEM = pl.BlockSpec(memory_space=pltpu.VMEM)
ANY = pl.BlockSpec(memory_space=pl.ANY)


def shards(counts, features, weights, biases):
    gx, gy, gz = (counts[a] for a in ("gx", "gy", "gz"))
    two_sided = gx != 2
    section = lax.axis_index("segment")
    micro, chans, depth, rows, lanes = features.shape
    mine = lax.dynamic_index_in_dim(features, section, 0, keepdims=False)

    def along_x(low, high):
        if not two_sided:
            return [lax.ppermute(low, "gx", swap_pairs(2))]
        up = [(i, i + 1) for i in range(gx - 1)]
        return [lax.ppermute(high, "gx", up), lax.ppermute(low, "gx", [(j, i) for i, j in up])]

    raws = along_x(mine, mine)
    tiles, edge_z, edge_a, edge_b = pl.pallas_call(
        pack_kernel,
        out_shape=(
            jax.ShapeDtypeStruct((depth, rows, chans, lanes), BF),
            jax.ShapeDtypeStruct((depth, chans, lanes), BF),
            jax.ShapeDtypeStruct((depth * WIDE, chans, lanes), BF),
            jax.ShapeDtypeStruct((depth * WIDE, chans, lanes), BF),
        ),
        in_specs=[VMEM],
        out_specs=(VMEM,) * 4,
        name="pack",
        cost_estimate=pl.CostEstimate(flops=4_000_000, bytes_accessed=2_000_000, transcendentals=0),
    )(mine)
    from_z = lax.ppermute(edge_z, "gz", swap_pairs(gz))
    from_a = lax.ppermute(jnp.concatenate([edge_a, from_z]), "gy", swap_pairs(gy))
    from_b = lax.ppermute(jnp.concatenate([edge_b, from_z]), "gy", shifted_pairs(gy))
    halo = jnp.concatenate([from_a, from_b, from_z])
    halos = along_x(halo, halo)

    table = pl.pallas_call(
        functools.partial(weight_kernel, not two_sided),
        out_shape=jax.ShapeDtypeStruct((2, 208, 256), BF),
        in_specs=[VMEM] * 2,
        out_specs=VMEM,
        name="weights",
        cost_estimate=pl.CostEstimate(flops=1_000_000, bytes_accessed=400_000, transcendentals=0),
    )(jnp.transpose(weights[0], (0, 3, 4, 5, 1, 2)), biases[0])
    other = lax.ppermute(table, "segment", swap_pairs(2))
    pair = jnp.stack([table, other])
    tables = jnp.where(section == 0, pair, pair[::-1]).reshape(4, 208, 256)

    ext = depth + (2 * WIDE if two_sided else WIDE)
    ext_rows = rows + 2 * WIDE
    per = -(-ext_rows * SEG // 128)
    per += per % 2
    keep, send = pl.pallas_call(
        functools.partial(main_kernel, two_sided, counts),
        out_shape=(
            jax.ShapeDtypeStruct((micro, chans, depth, rows, lanes), BF),
            jax.ShapeDtypeStruct((chans, depth, rows, lanes), BF),
        ),
        in_specs=[VMEM] * (3 + 2 * len(raws)),
        out_specs=(ANY, ANY),
        scratch_shapes=[
            pltpu.VMEM((ext + 2, ext_rows + 2, chans, lanes), BF),
            pltpu.VMEM((ext + 2, ext_rows + 2, chans, lanes), BF),
            pltpu.VMEM((ext + 2, per + 2, chans, lanes), BF),
            pltpu.VMEM((ext + 2, per + 2, chans, lanes), BF),
            pltpu.VMEM((4, 64, 128), F32),
            pltpu.VMEM((2, chans, depth, rows, lanes), BF),
            pltpu.SemaphoreType.DMA((2,)),
        ],
        name="layers",
        cost_estimate=pl.CostEstimate(flops=4_000_000_000, bytes_accessed=4_000_000, transcendentals=0),
    )(tiles, halo, *raws, *halos, tables)
    got = lax.ppermute(send, "segment", swap_pairs(2))
    return lax.dynamic_update_index_in_dim(keep, got, 1 - section, 0)[None]


def solution(mesh):
    placed = (
        P(None, None, "gx", "gy", "gz"),
        P("segment", None, None, None, None, None, None),
        P("segment", None, None),
    )
    return jax.shard_map(
        functools.partial(shards, dict(mesh.shape)),
        mesh=mesh,
        in_specs=placed,
        out_specs=P("segment", None, None, "gx", "gy", "gz"),
        check_vma=False,
    )
```

time: 195 us -> 46.9 us (0.24); the launches traced: 192 us -> 46.6 us
  matrix products: 45.5 us -> 0 us
  starting transfers between devices: 49.8 us -> 8.09 us
  waiting for transfers between devices: 47.8 us -> 14.3 us
  local copies, waits for them, and re-layouts: 32.2 us -> 3.81 us
  Pallas kernels: 0 us -> 18.5 us
  blocking collectives: 8.64 us -> 0 us
  other arithmetic: 6.92 us -> 1.77 us
    dot_general x40 -> x0, matrix products: 45.5 us -> none  [the longest x36 38.4 us: convolve(): jnp.einsum('oid,dixyz->oxyz', taps, slab, preferred_element_type=jnp.floa...]
    ppermute x24 -> x7, starting transfers between devices: 49.8 us -> 8.09 us  [the longest x1 2.99 us: shards(): from_z = lax.ppermute(edge_z, 'gz', swap_pairs(gz))]
    ppermute x24 -> x7, waiting for transfers between devices: 47.8 us -> 14.3 us  [the longest x2 10.1 us: along_x(): return [lax.ppermute(low, 'gx', swap_pairs(2))]]
    slice x20 -> x0, local copies, waits for them, and re-layouts: 23.2 us -> none  [the longest x4 15 us: convolve(): slab = shifted[:, :, step_x:step_x + depth, step_y:step_y + height, :]]
    pallas_call x0 -> x3, Pallas kernels: none -> 18.5 us  [the longest x1 14.2 us: shards(): pl.pallas_call(functools.partial(main_kernel, two_sided, counts), out_sha...]
    ppermute x8 -> x0, local copies, waits for them, and re-layouts: 6.48 us -> none  [the longest x4 3.24 us: with_halo(): after = lax.ppermute(initial, axis, down)]
    concatenate x7 -> x1, other arithmetic: 6.71 us -> 0.89 us  [shards(): jnp.concatenate([edge_b, from_z])]
    all_to_all x1 -> x0, blocking collectives: 4.71 us -> none  [shards(): lax.all_to_all(stacked, 'segment', split_axis=0, concat_axis=1, tiled=True)]
  transfers between devices with their start and end apart: 24 -> 7, of which waited for: 17 -> 4; matrix products, arithmetic and copies ran while one was open for 3% -> 2% of each run, Pallas kernels for 0% -> 4%
where the time goes in v1:
time: 46.9 us; the launch traced here: 46.6 us
  Pallas kernels  18.5 us (39%)
  waiting for transfers between devices  14.3 us (30%)
  starting transfers between devices  8.09 us (17%)
  local copies, waits for them, and re-layouts  3.81 us (8%)
  other arithmetic  1.77 us (4%)
    pallas_call x1, Pallas kernels, shards(): pl.pallas_call(functools.partial(main_kernel, two_sided, counts), out_sha...  14.2 us
    ppermute x2, waiting for transfers between devices, along_x(): return [lax.ppermute(low, 'gx', swap_pairs(2))]  10.1 us
    ppermute x1, starting transfers between devices, shards(): from_z = lax.ppermute(edge_z, 'gz', swap_pairs(gz))  2.99 us
    pallas_call x1, Pallas kernels, shards(): pl.pallas_call(pack_kernel, out_shape=(jax.ShapeDtypeStruct((depth, rows,...  2.36 us
    ppermute x1, starting transfers between devices, shards(): lax.ppermute(jnp.concatenate([edge_a, from_z]), 'gy', swap_pairs(gy))  2.14 us
    unnamed x14, local copies, waits for them, and re-layouts  2.12 us
    ppermute x1, waiting for transfers between devices, shards(): got = lax.ppermute(send, 'segment', swap_pairs(2))  2.1 us
    ppermute x2, starting transfers between devices, along_x(): return [lax.ppermute(low, 'gx', swap_pairs(2))]  2.09 us
  transfers between devices with their start and end apart: 7, of which 4 were waited for; matrix products, arithmetic and copies ran while one was open for 2% of the time, Pallas kernels for 4%

profile of v1, /device:TPU:0, one launch (start us, length us, event | category | flops | bytes accessed | tf_op | source)
XLA Modules:
  0.0 46.6 jit_solution(16797621656607974839)
XLA Ops:
  0.0 0.0 copy-start
  0.0 1.2 %copy-done = bf16[2,16,4,32,128]{4,3,2,1,0:T(8,128)(2,1)S(1)} copy-done((bf16[2,16,4,32,128]{4,3,2,1,0:T(8,128)(2,1)S(1)}, bf16[2,16,4,32,128]{4,3,2,1,0:T(8,128)(2,1)}, u32[]{:S(2)}) %copy-start) | copy-done | bytes 1048600
  1.2 0.8 %dynamic-slice_bitcast_fusion.x_ref = bf16[16,4,32,128]{3,2,1,0:T(8,128)(2,1)} fusion(bf16[2,16,4,32,128]{4,3,2,1,0:T(8,128)(2,1)S(1)} %copy-done, s32[]{:T(128)S(6)} %select_n.16), kind=kLoop, calls=%fused_computation.2 | loop fusion | bytes 1048580 | tf_op jit(solution)/shard_map/jit(dynamic_index_in_dim)/squeeze | solution.py:333
  2.1 0.0 copy-start.1
  2.1 2.4 %pack.1 = (bf16[4,32,16,128]{3,2,1,0:T(8,128)(2,1)}, bf16[4,16,128]{2,1,0:T(8,128)(2,1)}, bf16[16,16,128]{2,1,0:T(8,128)(2,1)}, bf16[16,16,128]{2,1,0:T(8,128)(2,1)}) custom-call(bf16[16,4,32,128]{3,2,1,0:T(8,128)(2,1)} %dynamic-slice_bitcast_fusion.x_ref), custom_call_target="tpu_custom_call" | custom-call | flops 4000000 | bytes 2000000 | tf_op jit(solution)/shard_map/pack/pallas_call | solution.py:342
  4.4 3.0 %collective-permute-start = (bf16[4,16,128]{2,1,0:T(8,128)(2,1)}, bf16[4,16,128]{2,1,0:T(8,128)(2,1)S(1)}, u32[]{:S(2)}, u32[]{:S(2)}) collective-permute-start(bf16[4,16,128]{2,1,0:T(8,128)(2,1)} %get-tuple-element.13), channel_id=1, source_target_pairs={{0,1},{1,0},{2,3},{3,2},{4,5},{5,4},{6,7},{7,6},{8,9},{9,8},{10,11... | collective-permute-start | bytes 49160 | tf_op jit(solution)/shard_map/ppermute | solution.py:355
  7.4 1.9 %collective-permute-done = bf16[4,16,128]{2,1,0:T(8,128)(2,1)S(1)} collective-permute-done((bf16[4,16,128]{2,1,0:T(8,128)(2,1)}, bf16[4,16,128]{2,1,0:T(8,128)(2,1)S(1)}, u32[]{:S(2)}, u32[]{:S(2)}) %collective-permute-start) | collective-permute-done | bytes 16416 | tf_op jit(solution)/shard_map/ppermute | solution.py:355
  9.3 0.9 %pad_maximum_fusion.1 = (bf16[20,16,128]{2,1,0:T(8,128)(2,1)S(1)}, bf16[20,16,128]{2,1,0:T(8,128)(2,1)S(1)}) fusion(bf16[4,16,128]{2,1,0:T(8,128)(2,1)S(1)} %collective-permute-done, bf16[16,16,128]{2,1,0:T(8,128)(2,1)} %get-tuple-element.14, bf16[16,16,128]{2,1,0:T(8,128)(2,1)} %get-tuple-element.12), kind=kLoop, calls=%fused_computation.4 | loop fusion | flops 81920 | bytes 311296 | tf_op jit(solution)/shard_map/concatenate | solution.py:357
  10.2 2.1 %collective-permute-start.1 = (bf16[20,16,128]{2,1,0:T(8,128)(2,1)S(1)}, bf16[20,16,128]{2,1,0:T(8,128)(2,1)S(1)}, u32[]{:S(2)}, u32[]{:S(2)}) collective-permute-start(bf16[20,16,128]{2,1,0:T(8,128)(2,1)S(1)} %get-tuple-element.18), channel_id=1, source_target_pairs={{0,2},{2,0},{4,6},{6,4},{1,3},{3,1},{5,7},{7,5},{8,10},{10,8},{12,... | collective-permute-start | bytes 245768 | tf_op jit(solution)/shard_map/ppermute | solution.py:356
  12.4 0.0 copy-done.1
  12.4 1.5 %collective-permute-start.3 = (bf16[16,4,32,128]{3,2,1,0:T(8,128)(2,1)S(1)}, bf16[16,4,32,128]{3,2,1,0:T(8,128)(2,1)S(1)}, u32[]{:S(2)}, u32[]{:S(2)}) collective-permute-start(bf16[16,4,32,128]{3,2,1,0:T(8,128)(2,1)S(1)} %copy-done.1), channel_id=1, source_target_pairs={{0,8},{8,0},{1,9},{9,1},{2,10},{10,2},{3,11},{11,3},{4,12},{12,4},... | collective-permute-start | bytes 1572872 | tf_op jit(solution)/shard_map/ppermute | solution.py:337
  13.9 2.0 %weights.1 = bf16[2,208,256]{2,1,0:T(8,128)(2,1)} custom-call(bf16[2,3,3,3,16,16]{5,4,3,2,1,0:T(8,128)(2,1)} %bitcast.14, bf16[2,16]{1,0:T(2,128)(2,1)} %bitcast.16), custom_call_target="tpu_custom_call" | custom-call | flops 1000000 | bytes 400000 | tf_op jit(solution)/shard_map/weights/pallas_call | solution.py:361
  15.8 0.0 copy-start.2
  15.8 0.0 collective-permute-start.5
  15.8 0.8 %collective-permute-start.2 = (bf16[20,16,128]{2,1,0:T(8,128)(2,1)S(1)}, bf16[20,16,128]{2,1,0:T(8,128)(2,1)S(1)}, u32[]{:S(2)}, u32[]{:S(2)}) collective-permute-start(bf16[20,16,128]{2,1,0:T(8,128)(2,1)S(1)} %get-tuple-element.17), channel_id=1, source_target_pairs={{2,4},{4,2},{3,5},{5,3},{10,12},{12,10},{11,13},{13,11},{18,20},{2... | collective-permute-start | bytes 245768 | tf_op jit(solution)/shard_map/ppermute | solution.py:357
  16.6 0.0 collective-permute-done.1
  16.7 0.0 collective-permute-done.2
  16.7 0.0 copy-start.3
  16.7 0.6 %collective-permute-start.4 = (bf16[44,16,128]{2,1,0:T(8,128)(2,1)S(1)}, bf16[44,16,128]{2,1,0:T(8,128)(2,1)S(1)}, u32[]{:S(2)}, u32[]{:S(2)}) collective-permute-start(bf16[44,16,128]{2,1,0:T(8,128)(2,1)S(1)} %constant_dynamic-update-slice_fusion.halo_ref), channel_id=1, source_target_pairs={{0,8},{8,0},{1,9},{9,1},{2,10},{10,2},{3,11},{11,3},{4,12},{12,4},... | collective-permute-start | bytes 540680 | tf_op jit(solution)/shard_map/ppermute | solution.py:337
  17.3 0.2 collective-permute-done.5
  17.5 0.0 copy-done.2
  17.6 0.0 copy-done.3
  17.6 0.8 %reverse_select_fusion = bf16[2,2,208,256]{3,2,1,0:T(8,128)(2,1)} fusion(bf16[2,2,208,256]{3,2,1,0:T(8,128)(2,1)S(1)} %pad_maximum_fusion, pred[]{:T(512)S(6)} %eq.3), kind=kLoop, calls=%fused_computation | loop fusion | flops 212992 | bytes 851969 | tf_op jit(solution)/shard_map/jit(_where)/select_n | solution.py:371
  18.4 10.1 %collective-permute-done.4.rest_1_ = bf16[44,16,128]{2,1,0:T(8,128)(2,1)S(1)} collective-permute-done((bf16[44,16,128]{2,1,0:T(8,128)(2,1)S(1)}, bf16[44,16,128]{2,1,0:T(8,128)(2,1)S(1)}, u32[]{:S(2)}, u32[]{:S(2)}) %collective-permute-start.4) | collective-permute-done | bytes 180256 | tf_op jit(solution)/shard_map/ppermute | solution.py:337
  28.5 0.0 copy-start.5
  28.5 0.0 collective-permute-done.3.rest_0_
  28.5 0.7 %copy-done.5 = bf16[44,16,128]{2,1,0:T(8,128)(2,1)} copy-done((bf16[44,16,128]{2,1,0:T(8,128)(2,1)}, bf16[44,16,128]{2,1,0:T(8,128)(2,1)S(1)}, u32[]{:S(2)}) %copy-start.5) | copy-done | bytes 180248
  29.2 0.2 copy-done.4
  29.4 14.2 %layers.1 = (bf16[2,16,4,32,128]{4,3,2,1,0:T(8,128)(2,1)}, bf16[16,4,32,128]{3,2,1,0:T(8,128)(2,1)}) custom-call(bf16[4,32,16,128]{3,2,1,0:T(8,128)(2,1)} %get-tuple-element.11.own_ref, bf16[44,16,128]{2,1,0:T(8,128)(2,1)} %copy-done.3, bf16[16,4,32,128]{3,2,1,0:T(8,128)(2,1)} %copy-done.4, bf16[44,16,128]{2,1,0:T(8,128)(2,1)} %copy-done.5, ...), custom_call_target="tpu_custom_call" | custom-call | flops 4000000000 | bytes 4000000 | tf_op jit(solution)/shard_map/layers/pallas_call | solution.py:377
  43.6 0.1 collective-permute-start.6
  43.7 2.1 %collective-permute-done.6 = bf16[16,4,32,128]{3,2,1,0:T(8,128)(2,1)S(1)} collective-permute-done((bf16[16,4,32,128]{3,2,1,0:T(8,128)(2,1)}, bf16[16,4,32,128]{3,2,1,0:T(8,128)(2,1)S(1)}, u32[]{:S(2)}, u32[]{:S(2)}) %collective-permute-start.6) | collective-permute-done | bytes 524320 | tf_op jit(solution)/shard_map/ppermute | solution.py:397
  45.8 0.8 %bitcast_dynamic-update-slice_fusion = bf16[1,2,16,4,32,128]{5,4,3,2,1,0:T(8,128)(2,1)} fusion(bf16[1,2,16,4,32,128]{5,4,3,2,1,0:T(8,128)(2,1)} %bitcast.17, s32[]{:T(128)S(6)} %select_n.19, bf16[16,4,32,128]{3,2,1,0:T(8,128)(2,1)S(1)} %collective-permute-done.6), kind=kLoop, calls=%fused_computation.1 | loop fusion | bytes 1048580 | tf_op jit(solution)/shard_map/jit(dynamic_update_index_in_dim)/dynamic_update_slice | solution.py:398
  (5 shorter events, 0.1 us)
Async XLA Ops:
  0.0 1.2 %copy-start = (bf16[2,16,4,32,128]{4,3,2,1,0:T(8,128)(2,1)S(1)}, bf16[2,16,4,32,128]{4,3,2,1,0:T(8,128)(2,1)}, u32[]{:S(2)}) copy-start(bf16[2,16,4,32,128]{4,3,2,1,0:T(8,128)(2,1)} %param.3) | copy-start | bytes 3145732
  2.1 10.3 %copy-start.1 = (bf16[16,4,32,128]{3,2,1,0:T(8,128)(2,1)S(1)}, bf16[16,4,32,128]{3,2,1,0:T(8,128)(2,1)}, u32[]{:S(2)}) copy-start(bf16[16,4,32,128]{3,2,1,0:T(8,128)(2,1)} %dynamic-slice_bitcast_fusion.x_ref) | copy-start | bytes 1572868
  4.4 4.9 %collective-permute-start = (bf16[4,16,128]{2,1,0:T(8,128)(2,1)}, bf16[4,16,128]{2,1,0:T(8,128)(2,1)S(1)}, u32[]{:S(2)}, u32[]{:S(2)}) collective-permute-start(bf16[4,16,128]{2,1,0:T(8,128)(2,1)} %get-tuple-element.13), channel_id=1, source_target_pairs={{0,1},{1,0},{2,3},{3,2},{4,5},{5,4},{6,7},{7,6},{8,9},{9,8},{10,11... | collective-permute-start | bytes 49160 | tf_op jit(solution)/shard_map/ppermute | solution.py:355
  10.2 6.4 %collective-permute-start.1 = (bf16[20,16,128]{2,1,0:T(8,128)(2,1)S(1)}, bf16[20,16,128]{2,1,0:T(8,128)(2,1)S(1)}, u32[]{:S(2)}, u32[]{:S(2)}) collective-permute-start(bf16[20,16,128]{2,1,0:T(8,128)(2,1)S(1)} %get-tuple-element.18), channel_id=1, source_target_pairs={{0,2},{2,0},{4,6},{6,4},{1,3},{3,1},{5,7},{7,5},{8,10},{10,8},{12,... | collective-permute-start | bytes 245768 | tf_op jit(solution)/shard_map/ppermute | solution.py:356
  12.4 16.1 %collective-permute-start.3 = (bf16[16,4,32,128]{3,2,1,0:T(8,128)(2,1)S(1)}, bf16[16,4,32,128]{3,2,1,0:T(8,128)(2,1)S(1)}, u32[]{:S(2)}, u32[]{:S(2)}) collective-permute-start(bf16[16,4,32,128]{3,2,1,0:T(8,128)(2,1)S(1)} %copy-done.1), channel_id=1, source_target_pairs={{0,8},{8,0},{1,9},{9,1},{2,10},{10,2},{3,11},{11,3},{4,12},{12,4},... | collective-permute-start | bytes 1572872 | tf_op jit(solution)/shard_map/ppermute | solution.py:337
  15.8 1.7 %copy-start.2 = (bf16[2,208,256]{2,1,0:T(8,128)(2,1)S(1)}, bf16[2,208,256]{2,1,0:T(8,128)(2,1)}, u32[]{:S(2)}) copy-start(bf16[2,208,256]{2,1,0:T(8,128)(2,1)} %weights.1) | copy-start | bytes 638980
  15.8 1.7 %collective-permute-start.5 = (bf16[2,208,256]{2,1,0:T(8,128)(2,1)}, bf16[2,208,256]{2,1,0:T(8,128)(2,1)S(1)}, u32[]{:S(2)}, u32[]{:S(2)}) collective-permute-start(bf16[2,208,256]{2,1,0:T(8,128)(2,1)} %weights.1), channel_id=1, source_target_pairs={{0,16},{16,0},{1,17},{17,1},{2,18},{18,2},{3,19},{19,3},{4,20},{20... | collective-permute-start | bytes 638984 | tf_op jit(solution)/shard_map/ppermute | solution.py:369
  15.8 0.8 %collective-permute-start.2 = (bf16[20,16,128]{2,1,0:T(8,128)(2,1)S(1)}, bf16[20,16,128]{2,1,0:T(8,128)(2,1)S(1)}, u32[]{:S(2)}, u32[]{:S(2)}) collective-permute-start(bf16[20,16,128]{2,1,0:T(8,128)(2,1)S(1)} %get-tuple-element.17), channel_id=1, source_target_pairs={{2,4},{4,2},{3,5},{5,3},{10,12},{12,10},{11,13},{13,11},{18,20},{2... | collective-permute-start | bytes 245768 | tf_op jit(solution)/shard_map/ppermute | solution.py:357
  16.7 0.9 %copy-start.3 = (bf16[44,16,128]{2,1,0:T(8,128)(2,1)}, bf16[44,16,128]{2,1,0:T(8,128)(2,1)S(1)}, u32[]{:S(2)}) copy-start(bf16[44,16,128]{2,1,0:T(8,128)(2,1)S(1)} %constant_dynamic-update-slice_fusion.halo_ref) | copy-start | bytes 540676
  16.7 11.8 %collective-permute-start.4 = (bf16[44,16,128]{2,1,0:T(8,128)(2,1)S(1)}, bf16[44,16,128]{2,1,0:T(8,128)(2,1)S(1)}, u32[]{:S(2)}, u32[]{:S(2)}) collective-permute-start(bf16[44,16,128]{2,1,0:T(8,128)(2,1)S(1)} %constant_dynamic-update-slice_fusion.halo_ref), channel_id=1, source_target_pairs={{0,8},{8,0},{1,9},{9,1},{2,10},{10,2},{3,11},{11,3},{4,12},{12,4},... | collective-permute-start | bytes 540680 | tf_op jit(solution)/shard_map/ppermute | solution.py:337
  28.5 0.7 %copy-start.5 = (bf16[44,16,128]{2,1,0:T(8,128)(2,1)}, bf16[44,16,128]{2,1,0:T(8,128)(2,1)S(1)}, u32[]{:S(2)}) copy-start(bf16[44,16,128]{2,1,0:T(8,128)(2,1)S(1)} %collective-permute-done.4.rest_1_) | copy-start | bytes 540676
  28.5 0.9 %copy-start.4 = (bf16[16,4,32,128]{3,2,1,0:T(8,128)(2,1)}, bf16[16,4,32,128]{3,2,1,0:T(8,128)(2,1)S(1)}, u32[]{:S(2)}) copy-start(bf16[16,4,32,128]{3,2,1,0:T(8,128)(2,1)S(1)} %collective-permute-done.3.rest_0_) | copy-start | bytes 1572868
  43.6 2.2 %collective-permute-start.6 = (bf16[16,4,32,128]{3,2,1,0:T(8,128)(2,1)}, bf16[16,4,32,128]{3,2,1,0:T(8,128)(2,1)S(1)}, u32[]{:S(2)}, u32[]{:S(2)}) collective-permute-start(bf16[16,4,32,128]{3,2,1,0:T(8,128)(2,1)} %get-tuple-element.16), channel_id=1, source_target_pairs={{0,16},{16,0},{1,17},{17,1},{2,18},{18,2},{3,19},{19,3},{4,20},{20... | collective-permute-start | bytes 1572872 | tf_op jit(solution)/shard_map/ppermute | solution.py:397

commit v2 on v1

v2 whole, which is shorter than its diff:
```python
import functools

import jax
import jax.numpy as jnp
from jax import lax
from jax.experimental import pallas as pl
from jax.experimental.pallas import tpu as pltpu
from jax.sharding import PartitionSpec as P


WIDE = 4
SEG = 16
BF = jnp.bfloat16
F32 = jnp.float32


def swap_pairs(size):
    return [(i, i ^ 1) for i in range(size) if i ^ 1 < size]


def shifted_pairs(size):
    return [(i, j) for i in range(1, size - 1, 2) for j in [i + 1]] + [
        (i + 1, i) for i in range(1, size - 1, 2)
    ]


def transposer():
    row = lax.broadcasted_iota(jnp.int32, (256, 256), 0)
    col = lax.broadcasted_iota(jnp.int32, (256, 256), 1)
    hit = ((row >> 4) == (col & 15)) & ((row & 15) == (col >> 4))
    return jnp.where(hit, 1.0, 0.0).astype(BF)


def lane_mask(test):
    lane = lax.broadcasted_iota(jnp.int32, (16, 128), 1)
    return jnp.where(test(lane), 1.0, 0.0).astype(BF)


def swap_rows(turn, blocks):
    wide = jnp.concatenate(blocks, 1) if len(blocks) > 1 else blocks[0]
    turned = jnp.dot(turn, wide, preferred_element_type=F32).astype(BF)
    return [turned[:, k * 128 : (k + 1) * 128].reshape(16, 16, 128) for k in range(len(blocks))]


def to_tiles(turn, ref, x, store):
    rows = ref.shape[2]
    starts = list(range(0, rows, 16))
    for k in range(0, len(starts), 2):
        some = starts[k : k + 2]
        for y0, block in zip(some, swap_rows(turn, [ref[:, x, y0 : y0 + 16, :].reshape(256, 128) for y0 in some])):
            store(y0, block)


def tile_kernel(x_hbm, tile_ref, x_ref, sems):
    depth = tile_ref.shape[0]
    section = lax.axis_index("segment")
    copies = [
        pltpu.make_async_copy(x_hbm.at[section, :, x], x_ref.at[:, x], sems.at[x]) for x in range(depth)
    ]
    for copy in copies:
        copy.start()
    turn = transposer()
    for x in range(depth):
        copies[x].wait()

        def store(y0, block):
            tile_ref[x, y0 : y0 + 16] = block

        to_tiles(turn, x_ref, x, store)


def pack_kernel(tile_ref, z_ref, a_ref, b_ref):
    depth, rows = tile_ref.shape[0], tile_ref.shape[1]
    right = lax.axis_index("gz") == 0
    even = lax.rem(lax.axis_index("gy"), 2) == 0
    turned_by = jnp.where(right, WIDE, 0)
    masks = [lane_mask(lambda lane: (((lane + turned_by) & 127) >> 2) == y) for y in range(rows)]
    for x in range(depth):
        parts = [jnp.zeros((16, 128), BF) for _ in range(4)]
        for y in range(rows):
            moved = pltpu.roll(tile_ref[x, y], 4 * y, 1) if y else tile_ref[x, y]
            parts[y % 4] = parts[y % 4] + moved * masks[y]
        total = (parts[0] + parts[1]) + (parts[2] + parts[3])
        z_ref[x] = pltpu.roll(total, turned_by, 1)
    first = jnp.where(even, rows - WIDE, 0)
    second = jnp.where(even, 0, rows - WIDE)
    for x in range(depth):
        a_ref[x * WIDE : (x + 1) * WIDE] = tile_ref[x, pl.ds(first, WIDE)]
        b_ref[x * WIDE : (x + 1) * WIDE] = tile_ref[x, pl.ds(second, WIDE)]


def weight_kernel(flip_x, w_ref, b_ref, t_ref):
    layers = w_ref.shape[0]
    zero = jnp.zeros((16, 16), BF)
    flipped = lax.axis_index("gx") == 1 if flip_x else None
    row = lax.broadcasted_iota(jnp.int32, (16, 16), 0)
    col = lax.broadcasted_iota(jnp.int32, (16, 16), 1)
    for layer in range(layers):
        for dz in range(3):
            for xo in range(2):
                for yo in range(2):
                    pieces = []
                    for xi in range(4):
                        for yi in range(4):
                            dx, dy = xi - xo, yi - yo
                            if 0 <= dx < 3 and 0 <= dy < 3:
                                at = jnp.where(flipped, 2 - dx, dx) if flip_x else dx
                                pieces.append(w_ref[layer, at, dy, dz])
                            else:
                                pieces.append(zero)
                    at_row = ((dz * 2 + xo) * 2 + yo) * 16
                    t_ref[layer, at_row : at_row + 16] = jnp.concatenate(pieces, 1)
        spread = jnp.broadcast_to(b_ref[layer : layer + 1, :].astype(F32), (16, 16))
        column = jnp.sum(jnp.where(row == col, spread, 0.0), axis=1, keepdims=True)
        t_ref[layer, 192:208] = jnp.broadcast_to(column, (16, 256)).astype(BF)


def layer_kernel(two_sided, counts, plan, n_raw, n_state, *refs):
    fills, steps, emits = plan
    raws, refs = refs[:n_raw], refs[n_raw:]
    halos, refs = refs[:n_raw], refs[n_raw:]
    mine_ref, other_ref = refs[:2]
    refs = refs[2 + n_state :]
    levels, strips, refs = refs[:4], refs[4:8], refs[8:]
    if emits:
        keep_ref, send_ref, t_ref, bias_ref, out_ref, sems = refs
    else:
        t_ref, bias_ref = refs
    depth, rows = raws[0].shape[0], raws[0].shape[1]
    ext_rows = rows + 2 * WIDE
    per = strips[0].shape[1] - 2
    segments = 128 // SEG
    blk = depth * WIDE + depth
    section = lax.axis_index("segment")
    gx, gy = lax.axis_index("gx"), lax.axis_index("gy")
    right = lax.axis_index("gz") == 0
    even = lax.rem(gy, 2) == 0
    top_ok = jnp.where(gy == 0, 0.0, 1.0).astype(F32)
    low_ok = jnp.where(gy == counts["gy"] - 1, 0.0, 1.0).astype(F32)
    prev_at = jnp.where(even, blk, 0)
    next_at = jnp.where(even, 0, blk)
    zero_tile = jnp.zeros((16, 128), BF)
    own_at = WIDE if two_sided else 0

    def flip(i):
        return i if two_sided else jnp.where(gx == 1, depth - 1 - i, i)

    if not n_state:
        for v, s in zip(levels, strips):
            for x in (0, 1):
                v[x] = jnp.zeros(v.shape[1:], BF)
                s[x] = jnp.zeros(s.shape[1:], BF)
        for x in range(2, levels[0].shape[0]):
            levels[0][x, 0] = zero_tile
            levels[0][x, ext_rows + 1] = zero_tile
            levels[2][x, 2] = zero_tile
            levels[2][x, ext_rows - 1] = zero_tile

    ahead = jnp.where(right, 3 * WIDE, 0)
    own_masks = [
        lane_mask(
            lambda lane: ((((lane + ahead) & 127) >> 4) == j) & (((lane + ahead) & 15) < 3 * WIDE)
        )
        for j in range(segments)
    ]
    halo_masks = [lane_mask(lambda lane: ((lane >> 4) == j) & ((lane & 15) < WIDE)) for j in range(segments)]
    own_turn = jnp.where(right, 3 * WIDE, WIDE)
    halo_turn = jnp.where(right, 3 * WIDE, 0)
    va, sa = levels[0], strips[0]

    for p, source, place in fills:
        i = flip(place)
        h = halos[source]
        q = p + 2
        va[q, 1 + WIDE : 1 + WIDE + rows] = raws[source][i]
        va[q, 1 : 1 + WIDE] = h[pl.ds(prev_at + i * WIDE, WIDE)]
        va[q, 1 + WIDE + rows : 1 + 2 * WIDE + rows] = h[pl.ds(next_at + i * WIDE, WIDE)]
        edge_prev = h[prev_at + depth * WIDE + i]
        edge_own = h[2 * blk + i]
        edge_next = h[next_at + depth * WIDE + i]
        for yo in range(per):
            own_sum, halo_sum = zero_tile, zero_tile
            for j in range(segments):
                r = per * j + yo
                if r >= ext_rows:
                    continue
                row = va[q, 1 + r]
                own_sum = own_sum + (pltpu.roll(row, SEG * j, 1) if j else row) * own_masks[j]
                if r < WIDE:
                    edge, lane = edge_prev, WIDE * (rows - WIDE + r)
                elif r < WIDE + rows:
                    edge, lane = edge_own, WIDE * (r - WIDE)
                else:
                    edge, lane = edge_next, WIDE * (r - WIDE - rows)
                by = (SEG * j - lane) % 128
                halo_sum = halo_sum + (pltpu.roll(edge, by, 1) if by else edge) * halo_masks[j]
            sa[q, 1 + yo] = pltpu.roll(own_sum, own_turn, 1) + pltpu.roll(halo_sum, halo_turn, 1)
        sa[q, 0] = pltpu.roll(sa[q, per], SEG, 1)
        sa[q, per + 1] = pltpu.roll(sa[q, 1], 128 - SEG, 1)

    for layer in range(2):
        t_ref[2 * section + layer] = mine_ref[layer]
        t_ref[2 * (1 - section) + layer] = other_ref[layer]
    for layer in range(4):
        one = t_ref[layer, 192:208, :128].astype(F32)
        for k in range(4):
            bias_ref[layer, 16 * k : 16 * (k + 1)] = one

    wide_lane = lax.broadcasted_iota(jnp.int32, (64, 128), 1)
    not_first = jnp.where(wide_lane == 0, 0.0, 1.0)
    not_last = jnp.where(wide_lane == 127, 0.0, 1.0)
    strip_lane = lax.broadcasted_iota(jnp.int32, (16, 128), 1) >> 4

    def strip_ok(yo):
        r = strip_lane * per + yo
        return jnp.where(r < WIDE, top_ok, jnp.where(r >= WIDE + rows, low_ok, 1.0))

    def group(layer, at):
        src, ssrc = levels[layer], strips[layer]
        last = layer == 3
        dst, sdst = (levels[0], strips[0]) if last else (levels[layer + 1], strips[layer + 1])
        r0, row_groups = ((0, ext_rows // 2), (2, ext_rows // 2 - 2), (2, ext_rows // 2 - 2), (WIDE, rows // 2))[layer]
        items = [(src, r0 + 2 * k, False) for k in range(row_groups)]
        items += [(ssrc, 2 * k, True) for k in range(per // 2)]
        half = len(items) // 2
        order = [[items[k], items[half + k]] for k in range(half)] + [[t] for t in items[2 * half :]]
        for pair in order:
            columns = [
                jnp.concatenate([ref[at + 1 + xi, r : r + 4].reshape(64, 128) for xi in range(4)], 0)
                for ref, r, _ in pair
            ]
            wide = jnp.concatenate(columns, 1) if len(columns) > 1 else columns[0]
            got = jnp.dot(t_ref[layer, :192], wide, preferred_element_type=F32)
            for k, (_, r, strip) in enumerate(pair):
                part = got[:, 128 * k : 128 * (k + 1)]
                a = part[64:128] + pltpu.roll(part[:64], 1, 1) * not_first
                a = a + pltpu.roll(part[128:], 127, 1) * not_last
                a = a + bias_ref[layer]
                a = jnp.maximum(a, 0.2 * a)
                for xo in range(2):
                    place = at + xo
                    if isinstance(place, int) and place < 0:
                        continue
                    for yo in range(2):
                        one = a[(2 * xo + yo) * 16 : (2 * xo + yo + 1) * 16]
                        if not last:
                            if strip:
                                one = one * strip_ok(r + yo)
                            elif r + yo < WIDE:
                                one = one * top_ok
                            elif r + yo >= WIDE + rows:
                                one = one * low_ok
                            if two_sided:
                                outside = ((place < WIDE) & (gx == 0)) | (
                                    (place >= WIDE + depth) & (gx == counts["gx"] - 1)
                                )
                                one = one * jnp.where(outside, 0.0, 1.0)
                        one = one.astype(BF)
                        if strip:
                            sdst[place + 2, r + yo + 1] = one
                            if r + yo == 0:
                                sdst[place + 2, per + 1] = pltpu.roll(one, 128 - SEG, 1)
                            if r + yo == per - 1:
                                sdst[place + 2, 0] = pltpu.roll(one, SEG, 1)
                        else:
                            dst[place + 2, r + yo + 1] = one

    def emit(part, places):
        turn = transposer()
        edge_turn = jnp.where(right, 0, 2 * WIDE)
        edge_ahead = jnp.where(right, WIDE, 0)
        edge_mask = lane_mask(lambda lane: ((lane + edge_ahead) & 127) < WIDE)
        inner_mask = lane_mask(lambda lane: ((lane + edge_ahead) & 127) >= WIDE)
        v, s = (levels[2], strips[2]) if part == 0 else (levels[0], strips[0])
        for i in places:
            p = own_at + i
            to = flip(i)
            starts = list(range(0, rows, 16))
            for k in range(0, len(starts), 2):
                some = starts[k : k + 2]
                blocks = []
                for y0 in some:
                    tiles = []
                    for y in range(y0, y0 + 16):
                        r = y + WIDE
                        j, yo = r // per, r % per
                        by = (128 - 3 * WIDE - SEG * j) % 128
                        edge = pltpu.roll(s[p + 2, yo + 1], by + edge_turn, 1)
                        tiles.append(v[p + 2, r + 1] * inner_mask + edge * edge_mask)
                    blocks.append(jnp.concatenate(tiles, 0))
                for y0, block in zip(some, swap_rows(turn, blocks)):
                    out_ref[part, :, to, y0 : y0 + 16] = block

    def copies(part):
        return (
            pltpu.make_async_copy(out_ref.at[part], keep_ref.at[section], sems.at[part]),
            pltpu.make_async_copy(out_ref.at[part], send_ref, sems.at[part]),
        )

    def move(part, finish):
        keep, send = copies(part)

        @pl.when(section == part)
        def _():
            (keep.wait if finish else keep.start)()

        @pl.when(section != part)
        def _():
            (send.wait if finish else send.start)()

    for step in steps:
        if step[0] == "emit":
            emit(step[1], range(depth))
            move(step[1], False)
        elif step[0] == "loop":
            _, layer, x0, n = step

            def body(g, carry):
                group(layer, x0 + 2 * g)
                return carry

            lax.fori_loop(0, n, body, 0)
        else:
            group(*step[1:])
    if emits:
        for part in range(2):
            move(part, True)


VMEM = pl.BlockSpec(memory_space=pltpu.VMEM)
ANY = pl.BlockSpec(memory_space=pl.ANY)


def shards(counts, features, weights, biases):
    gx, gy, gz = (counts[a] for a in ("gx", "gy", "gz"))
    two_sided = gx != 2
    section = lax.axis_index("segment")
    micro, chans, depth, rows, lanes = features.shape
    tiles = pl.pallas_call(
        tile_kernel,
        out_shape=jax.ShapeDtypeStruct((depth, rows, chans, lanes), BF),
        in_specs=[pl.BlockSpec(memory_space=pltpu.HBM)],
        out_specs=VMEM,
        scratch_shapes=[
            pltpu.VMEM((chans, depth, rows, lanes), BF),
            pltpu.SemaphoreType.DMA((depth,)),
        ],
        name="tiles",
        compiler_params=pltpu.CompilerParams(vmem_limit_bytes=4 << 20),
        cost_estimate=pl.CostEstimate(flops=4_000_000, bytes_accessed=1_000_000, transcendentals=0),
    )(features)

    def along_x(low, high):
        if not two_sided:
            return [lax.ppermute(low, "gx", swap_pairs(2))]
        up = [(i, i + 1) for i in range(gx - 1)]
        return [lax.ppermute(high, "gx", up), lax.ppermute(low, "gx", [(j, i) for i, j in up])]

    raws = along_x(tiles, tiles)
    edge_z, edge_a, edge_b = pl.pallas_call(
        pack_kernel,
        out_shape=(
            jax.ShapeDtypeStruct((depth, chans, lanes), BF),
            jax.ShapeDtypeStruct((depth * WIDE, chans, lanes), BF),
            jax.ShapeDtypeStruct((depth * WIDE, chans, lanes), BF),
        ),
        in_specs=[VMEM],
        out_specs=(VMEM,) * 3,
        name="pack",
        compiler_params=pltpu.CompilerParams(vmem_limit_bytes=4 << 20),
        cost_estimate=pl.CostEstimate(flops=4_000_000, bytes_accessed=1_000_000, transcendentals=0),
    )(tiles)
    from_z = lax.ppermute(edge_z, "gz", swap_pairs(gz))
    from_b = lax.ppermute(jnp.concatenate([edge_b, from_z]), "gy", shifted_pairs(gy))
    from_a = lax.ppermute(jnp.concatenate([edge_a, from_z]), "gy", swap_pairs(gy))
    halo = jnp.concatenate([from_a, from_b, from_z])
    halos = along_x(halo, halo)

    table = pl.pallas_call(
        functools.partial(weight_kernel, not two_sided),
        out_shape=jax.ShapeDtypeStruct((2, 208, 256), BF),
        in_specs=[VMEM] * 2,
        out_specs=VMEM,
        name="weights",
        compiler_params=pltpu.CompilerParams(vmem_limit_bytes=4 << 20),
        cost_estimate=pl.CostEstimate(flops=1_000_000, bytes_accessed=400_000, transcendentals=0),
    )(jnp.transpose(weights[0], (0, 3, 4, 5, 1, 2)), biases[0])
    other = lax.ppermute(table, "segment", swap_pairs(2))
    ext = depth + (2 * WIDE if two_sided else WIDE)
    ext_rows = rows + 2 * WIDE
    per = -(-ext_rows * SEG // 128)
    per += per % 2
    state = [jax.ShapeDtypeStruct((ext + 2, ext_rows + 2, chans, lanes), BF)] * 4
    state += [jax.ShapeDtypeStruct((ext + 2, per + 2, chans, lanes), BF)] * 4
    results = [
        jax.ShapeDtypeStruct((micro, chans, depth, rows, lanes), BF),
        jax.ShapeDtypeStruct((chans, depth, rows, lanes), BF),
    ]

    def stage(plan, blocks, edges, before):
        _, _, emits = plan
        n = len(blocks)
        return pl.pallas_call(
            functools.partial(layer_kernel, two_sided, counts, plan, n, len(before)),
            out_shape=state + (results if emits else []),
            in_specs=[VMEM] * (2 * n + 2 + len(before)),
            out_specs=[VMEM] * 8 + ([ANY, ANY] if emits else []),
            scratch_shapes=[pltpu.VMEM((4, 208, 256), BF), pltpu.VMEM((4, 64, 128), F32)]
            + ([pltpu.VMEM((2, chans, depth, rows, lanes), BF), pltpu.SemaphoreType.DMA((2,))] if emits else []),
            input_output_aliases={2 * n + 2 + k: k for k in range(len(before))},
            compiler_params=pltpu.CompilerParams(vmem_limit_bytes=24 << 20),
            cost_estimate=pl.CostEstimate(flops=2_000_000_000, bytes_accessed=4_000_000, transcendentals=0),
        )(*blocks, *edges, table, other, *before)

    def chain(k):
        return [("one", layer, 2 * k - 1 - layer) for layer in range(4) if 2 * k - layer >= 0]

    if two_sided:
        fills = [(p, 1, depth - WIDE + p) for p in range(WIDE)]
        fills += [(WIDE + p, 0, p) for p in range(depth)]
        fills += [(WIDE + depth + p, 2, p) for p in range(WIDE)]
        steps = []
        for layer in range(4):
            steps.append(("loop", layer, layer + 1, (ext - 2 * layer - 2) // 2))
            if layer % 2:
                steps.append(("emit", layer // 2))
        *_, keep, send = stage((fills, steps, True), [tiles, *raws], [halo, *halos], [])
    else:
        near = [(p, 0, p) for p in range(depth)]
        early = stage((near, chain(0) + chain(1), False), [tiles], [halo], [])
        far = [(depth + p, 0, p) for p in range(WIDE)]
        steps = chain(2) + [("emit", 0)] + chain(3) + [("emit", 1)]
        *_, keep, send = stage((far, steps, True), raws, halos, early)
    got = lax.ppermute(send, "segment", swap_pairs(2))
    return lax.dynamic_update_index_in_dim(keep, got, 1 - section, 0)[None]


def solution(mesh):
    placed = (
        P(None, None, "gx", "gy", "gz"),
        P("segment", None, None, None, None, None, None),
        P("segment", None, None),
    )

    def step(*args):
        return shards(dict(mesh.shape), *args)

    return jax.shard_map(
        step,
        mesh=mesh,
        in_specs=placed,
        out_specs=P("segment", None, None, "gx", "gy", "gz"),
        check_vma=False,
    )
```

time: 46.9 us -> 35.2 us (0.75)
  Pallas kernels: 18.5 us -> 11.4 us
  waiting for transfers between devices: 14.3 us -> 12.2 us
  other arithmetic: 1.77 us -> 0.01 us
  local copies, waits for them, and re-layouts: 3.81 us -> 2.1 us
  starting transfers between devices: 8.09 us -> 9.25 us
    pallas_call x2 -> x4, Pallas kernels: 16.6 us -> 11 us  [the longest x2 9.7 us: stage(): pl.pallas_call(functools.partial(layer_kernel, two_sided, counts, plan, n...]
    pallas_call x1, Pallas kernels: 1.95 us -> 0.33 us  [shards(): pl.pallas_call(functools.partial(weight_kernel, not two_sided), out_shape...]
    ppermute x2, waiting for transfers between devices: 10.1 us -> 8.55 us  [along_x(): return [lax.ppermute(low, 'gx', swap_pairs(2))]]
    ppermute x2, starting transfers between devices: 2.09 us -> 3.3 us  [along_x(): return [lax.ppermute(low, 'gx', swap_pairs(2))]]
    concatenate x1, other arithmetic: 0.89 us -> 0.01 us  [shards(): jnp.concatenate([edge_b, from_z])]
    unnamed x14 -> x8, local copies, waits for them, and re-layouts: 2.12 us -> 1.25 us
    select_n x1 -> x0, other arithmetic: 0.84 us -> none  [shards(): tables = jnp.where(section == 0, pair, pair[::-1]).reshape(4, 208, 256)]
    squeeze x1 -> x0, local copies, waits for them, and re-layouts: 0.84 us -> none  [shards(): mine = lax.dynamic_index_in_dim(features, section, 0, keepdims=False)]
  transfers between devices with their start and end apart: 7 -> 7, of which waited for: 4 -> 3; matrix products, arithmetic and copies ran while one was open for 2% -> 0% of each run, Pallas kernels for 4% -> 10%
where the time goes in v2:
time: 35.2 us; the launch traced here: 35 us
  waiting for transfers between devices  12.2 us (35%)
  Pallas kernels  11.4 us (32%)
  starting transfers between devices  9.25 us (26%)
  local copies, waits for them, and re-layouts  2.1 us (6%)
    pallas_call x2, Pallas kernels, stage(): pl.pallas_call(functools.partial(layer_kernel, two_sided, counts, plan, n...  9.7 us
    ppermute x2, waiting for transfers between devices, along_x(): return [lax.ppermute(low, 'gx', swap_pairs(2))]  8.55 us
    ppermute x2, starting transfers between devices, along_x(): return [lax.ppermute(low, 'gx', swap_pairs(2))]  3.3 us
    ppermute x1, starting transfers between devices, shards(): from_z = lax.ppermute(edge_z, 'gz', swap_pairs(gz))  3 us
    ppermute x1, starting transfers between devices, shards(): lax.ppermute(jnp.concatenate([edge_a, from_z]), 'gy', swap_pairs(gy))  2.14 us
    ppermute x1, waiting for transfers between devices, shards(): got = lax.ppermute(send, 'segment', swap_pairs(2))  1.89 us
    ppermute x1, waiting for transfers between devices, shards(): from_z = lax.ppermute(edge_z, 'gz', swap_pairs(gz))  1.72 us
    unnamed x8, local copies, waits for them, and re-layouts  1.25 us
  transfers between devices with their start and end apart: 7, of which 3 were waited for; matrix products, arithmetic and copies ran while one was open for 0% of the time, Pallas kernels for 10%

profile of v2, /device:TPU:0, one launch (start us, length us, event | category | flops | bytes accessed | tf_op | source)
XLA Modules:
  0.0 35.0 jit_solution(12098514007739219120)
XLA Ops:
  0.0 0.0 copy-start
  0.0 1.2 %copy-done = bf16[2,16,4,32,128]{4,3,2,1,0:T(8,128)(2,1)S(1)} copy-done((bf16[2,16,4,32,128]{4,3,2,1,0:T(8,128)(2,1)S(1)}, bf16[2,16,4,32,128]{4,3,2,1,0:T(8,128)(2,1)}, u32[]{:S(2)}) %copy-start) | copy-done | bytes 1048600
  1.2 0.0 copy-start.1
  1.2 0.0 copy-start.2
  1.2 1.0 %tiles.1.tile_ref.refs_0_ = bf16[4,32,16,128]{3,2,1,0:T(8,128)(2,1)S(1)} custom-call(bf16[2,16,4,32,128]{4,3,2,1,0:T(8,128)(2,1)S(1)} %copy-done), custom_call_target="tpu_custom_call" | custom-call | flops 4000000 | bytes 1000000 | tf_op jit(solution)/shard_map/tiles/pallas_call | solution.py:339
  2.3 0.3 pack.1
  2.6 3.0 %collective-permute-start.1 = (bf16[4,16,128]{2,1,0:T(8,128)(2,1)S(1)}, bf16[4,16,128]{2,1,0:T(8,128)(2,1)S(1)}, u32[]{:S(2)}, u32[]{:S(2)}) collective-permute-start(bf16[4,16,128]{2,1,0:T(8,128)(2,1)S(1)} %get-tuple-element.19), channel_id=1, source_target_pairs={{0,1},{1,0},{2,3},{3,2},{4,5},{5,4},{6,7},{7,6},{8,9},{9,8},{10,11... | collective-permute-start | bytes 49160 | tf_op jit(solution)/shard_map/ppermute | solution.py:373
  5.6 1.7 %collective-permute-done.1 = bf16[4,16,128]{2,1,0:T(8,128)(2,1)S(1)} collective-permute-done((bf16[4,16,128]{2,1,0:T(8,128)(2,1)S(1)}, bf16[4,16,128]{2,1,0:T(8,128)(2,1)S(1)}, u32[]{:S(2)}, u32[]{:S(2)}) %collective-permute-start.1) | collective-permute-done | bytes 16416 | tf_op jit(solution)/shard_map/ppermute | solution.py:373
  7.3 2.1 %collective-permute-start.2 = (bf16[20,16,128]{2,1,0:T(8,128)(2,1)S(1)}, bf16[20,16,128]{2,1,0:T(8,128)(2,1)S(1)}, u32[]{:S(2)}, u32[]{:S(2)}) collective-permute-start(bf16[20,16,128]{2,1,0:T(8,128)(2,1)S(1)} %get-tuple-element.32), channel_id=1, source_target_pairs={{0,2},{2,0},{4,6},{6,4},{1,3},{3,1},{5,7},{7,5},{8,10},{10,8},{12,... | collective-permute-start | bytes 245768 | tf_op jit(solution)/shard_map/ppermute | solution.py:375
  9.5 1.5 %collective-permute-start = (bf16[4,32,16,128]{3,2,1,0:T(8,128)(2,1)S(1)}, bf16[4,32,16,128]{3,2,1,0:T(8,128)(2,1)S(1)}, u32[]{:S(2)}, u32[]{:S(2)}) collective-permute-start(bf16[4,32,16,128]{3,2,1,0:T(8,128)(2,1)S(1)} %tiles.1.tile_ref.refs_0_), channel_id=1, source_target_pairs={{0,8},{8,0},{1,9},{9,1},{2,10},{10,2},{3,11},{11,3},{4,12},{12,4},... | collective-permute-start | bytes 1572872 | tf_op jit(solution)/shard_map/ppermute | solution.py:355
  10.9 0.0 copy-done.1
  10.9 0.0 copy-done.2
  10.9 0.3 weights.1.refs_2_
  11.3 0.1 collective-permute-start.5
  11.4 0.7 %collective-permute-start.3 = (bf16[20,16,128]{2,1,0:T(8,128)(2,1)S(1)}, bf16[20,16,128]{2,1,0:T(8,128)(2,1)S(1)}, u32[]{:S(2)}, u32[]{:S(2)}) collective-permute-start(bf16[20,16,128]{2,1,0:T(8,128)(2,1)S(1)} %get-tuple-element.31), channel_id=1, source_target_pairs={{2,4},{4,2},{3,5},{5,3},{10,12},{12,10},{11,13},{13,11},{18,20},{2... | collective-permute-start | bytes 245768 | tf_op jit(solution)/shard_map/ppermute | solution.py:374
  12.0 0.0 collective-permute-done.2
  12.1 0.0 collective-permute-done.3
  12.1 1.8 %collective-permute-start.4 = (bf16[44,16,128]{2,1,0:T(8,128)(2,1)S(1)}, bf16[44,16,128]{2,1,0:T(8,128)(2,1)S(1)}, u32[]{:S(2)}, u32[]{:S(2)}) collective-permute-start(bf16[44,16,128]{2,1,0:T(8,128)(2,1)S(1)} %constant_dynamic-update-slice_fusion.refs_1_), channel_id=1, source_target_pairs={{0,8},{8,0},{1,9},{9,1},{2,10},{10,2},{3,11},{11,3},{4,12},{12,4},... | collective-permute-start | bytes 540680 | tf_op jit(solution)/shard_map/ppermute | solution.py:355
  13.9 0.0 collective-permute-done.5.refs_3_
  13.9 3.1 %shard_map.37 = (bf16[10,42,16,128]{3,2,1,0:T(8,128)(2,1)S(1)}, bf16[10,42,16,128]{3,2,1,0:T(8,128)(2,1)S(1)}, bf16[10,42,16,128]{3,2,1,0:T(8,128)(2,1)S(1)}, bf...) custom-call(bf16[4,32,16,128]{3,2,1,0:T(8,128)(2,1)S(1)} %tiles.1.ti, ...), custom_call_target="tpu_custom_call" | custom-call | flops 2000000000 | bytes 4000000 | tf_op jit(solution)/shard_map/pallas_call | solution.py:403
  17.0 8.5 %collective-permute-done.4.refs_1_ = bf16[44,16,128]{2,1,0:T(8,128)(2,1)S(1)} collective-permute-done((bf16[44,16,128]{2,1,0:T(8,128)(2,1)S(1)}, bf16[44,16,128]{2,1,0:T(8,128)(2,1)S(1)}, u32[]{:S(2)}, u32[]{:S(2)}) %collective-permute-start.4) | collective-permute-done | bytes 180256 | tf_op jit(solution)/shard_map/ppermute | solution.py:355
  25.6 0.0 collective-permute-done.refs_0_
  25.6 6.6 %shard_map.38 = (bf16[10,42,16,128]{3,2,1,0:T(8,128)(2,1)S(1)}, bf16[10,42,16,128]{3,2,1,0:T(8,128)(2,1)S(1)}, bf16[10,42,16,128]{3,2,1,0:T(8,128)(2,1)S(1)}, bf...) custom-call(bf16[4,32,16,128]{3,2,1,0:T(8,128)(2,1)S(1)} %collective, ...), custom_call_target="tpu_custom_call", output_to_operand_aliasing={{0}: (4, {}), {1}: (5, {}), {2}: (6, {}), {3}: (7, {}), {4}... | custom-call | flops 2000000000 | bytes 4000000 | tf_op jit(solution)/shard_map/pallas_call | solution.py:403
  32.2 0.1 collective-permute-start.6
  32.3 1.9 %collective-permute-done.6 = bf16[16,4,32,128]{3,2,1,0:T(8,128)(2,1)S(1)} collective-permute-done((bf16[16,4,32,128]{3,2,1,0:T(8,128)(2,1)S(1)}, bf16[16,4,32,128]{3,2,1,0:T(8,128)(2,1)S(1)}, u32[]{:S(2)}, u32[]{:S(2)}) %collective-permute-start.6) | collective-permute-done | bytes 524320 | tf_op jit(solution)/shard_map/ppermute | solution.py:434
  34.2 0.8 %bitcast_dynamic-update-slice_fusion = bf16[1,2,16,4,32,128]{5,4,3,2,1,0:T(8,128)(2,1)} fusion(bf16[1,2,16,4,32,128]{5,4,3,2,1,0:T(8,128)(2,1)} %bitcast.9, s32[]{:T(128)S(6)} %select_n.4, bf16[16,4,32,128]{3,2,1,0:T(8,128)(2,1)S(1)} %collective-permute-done.6), kind=kLoop, calls=%fused_computation | loop fusion | bytes 1048580 | tf_op jit(solution)/shard_map/jit(dynamic_update_index_in_dim)/dynamic_update_slice | solution.py:435
  (4 shorter events, 0.0 us)
Async XLA Ops:
  0.0 1.2 %copy-start = (bf16[2,16,4,32,128]{4,3,2,1,0:T(8,128)(2,1)S(1)}, bf16[2,16,4,32,128]{4,3,2,1,0:T(8,128)(2,1)}, u32[]{:S(2)}) copy-start(bf16[2,16,4,32,128]{4,3,2,1,0:T(8,128)(2,1)} %x_hbm.1) | copy-start | bytes 3145732
  1.2 9.7 %copy-start.1 = (bf16[1,2,16,16,3,3,3]{3,2,6,5,4,1,0:T(8,128)(2,1)S(1)}, bf16[1,2,16,16,3,3,3]{3,2,6,5,4,1,0:T(8,128)(2,1)}, u32[]{:S(2)}) copy-start(bf16[1,2,16,16,3,3,3]{3,2,6,5,4,1,0:T(8,128)(2,1)} %param.4) | copy-start | bytes 82948
  1.2 9.7 %copy-start.2 = (bf16[1,2,16]{2,1,0:T(2,128)(2,1)S(1)}, bf16[1,2,16]{2,1,0:T(2,128)(2,1)}, u32[]{:S(2)}) copy-start(bf16[1,2,16]{2,1,0:T(2,128)(2,1)} %param.5) | copy-start | bytes 196
  2.6 4.7 %collective-permute-start.1 = (bf16[4,16,128]{2,1,0:T(8,128)(2,1)S(1)}, bf16[4,16,128]{2,1,0:T(8,128)(2,1)S(1)}, u32[]{:S(2)}, u32[]{:S(2)}) collective-permute-start(bf16[4,16,128]{2,1,0:T(8,128)(2,1)S(1)} %get-tuple-element.19), channel_id=1, source_target_pairs={{0,1},{1,0},{2,3},{3,2},{4,5},{5,4},{6,7},{7,6},{8,9},{9,8},{10,11... | collective-permute-start | bytes 49160 | tf_op jit(solution)/shard_map/ppermute | solution.py:373
  7.3 4.7 %collective-permute-start.2 = (bf16[20,16,128]{2,1,0:T(8,128)(2,1)S(1)}, bf16[20,16,128]{2,1,0:T(8,128)(2,1)S(1)}, u32[]{:S(2)}, u32[]{:S(2)}) collective-permute-start(bf16[20,16,128]{2,1,0:T(8,128)(2,1)S(1)} %get-tuple-element.32), channel_id=1, source_target_pairs={{0,2},{2,0},{4,6},{6,4},{1,3},{3,1},{5,7},{7,5},{8,10},{10,8},{12,... | collective-permute-start | bytes 245768 | tf_op jit(solution)/shard_map/ppermute | solution.py:375
  9.5 16.1 %collective-permute-start = (bf16[4,32,16,128]{3,2,1,0:T(8,128)(2,1)S(1)}, bf16[4,32,16,128]{3,2,1,0:T(8,128)(2,1)S(1)}, u32[]{:S(2)}, u32[]{:S(2)}) collective-permute-start(bf16[4,32,16,128]{3,2,1,0:T(8,128)(2,1)S(1)} %tiles.1.tile_ref.refs_0_), channel_id=1, source_target_pairs={{0,8},{8,0},{1,9},{9,1},{2,10},{10,2},{3,11},{11,3},{4,12},{12,4},... | collective-permute-start | bytes 1572872 | tf_op jit(solution)/shard_map/ppermute | solution.py:355
  11.3 2.6 %collective-permute-start.5 = (bf16[2,208,256]{2,1,0:T(8,128)(2,1)S(1)}, bf16[2,208,256]{2,1,0:T(8,128)(2,1)S(1)}, u32[]{:S(2)}, u32[]{:S(2)}) collective-permute-start(bf16[2,208,256]{2,1,0:T(8,128)(2,1)S(1)} %weights.1.refs_2_), channel_id=1, source_target_pairs={{0,16},{16,0},{1,17},{17,1},{2,18},{18,2},{3,19},{19,3},{4,20},{20... | collective-permute-start | bytes 638984 | tf_op jit(solution)/shard_map/ppermute | solution.py:388
  11.4 0.7 %collective-permute-start.3 = (bf16[20,16,128]{2,1,0:T(8,128)(2,1)S(1)}, bf16[20,16,128]{2,1,0:T(8,128)(2,1)S(1)}, u32[]{:S(2)}, u32[]{:S(2)}) collective-permute-start(bf16[20,16,128]{2,1,0:T(8,128)(2,1)S(1)} %get-tuple-element.31), channel_id=1, source_target_pairs={{2,4},{4,2},{3,5},{5,3},{10,12},{12,10},{11,13},{13,11},{18,20},{2... | collective-permute-start | bytes 245768 | tf_op jit(solution)/shard_map/ppermute | solution.py:374
  12.1 13.4 %collective-permute-start.4 = (bf16[44,16,128]{2,1,0:T(8,128)(2,1)S(1)}, bf16[44,16,128]{2,1,0:T(8,128)(2,1)S(1)}, u32[]{:S(2)}, u32[]{:S(2)}) collective-permute-start(bf16[44,16,128]{2,1,0:T(8,128)(2,1)S(1)} %constant_dynamic-update-slice_fusion.refs_1_), channel_id=1, source_target_pairs={{0,8},{8,0},{1,9},{9,1},{2,10},{10,2},{3,11},{11,3},{4,12},{12,4},... | collective-permute-start | bytes 540680 | tf_op jit(solution)/shard_map/ppermute | solution.py:355
  32.2 2.0 %collective-permute-start.6 = (bf16[16,4,32,128]{3,2,1,0:T(8,128)(2,1)S(1)}, bf16[16,4,32,128]{3,2,1,0:T(8,128)(2,1)S(1)}, u32[]{:S(2)}, u32[]{:S(2)}) collective-permute-start(bf16[16,4,32,128]{3,2,1,0:T(8,128)(2,1)S(1)} %get-tuple-element.30), channel_id=1, source_target_pairs={{0,16},{16,0},{1,17},{17,1},{2,18},{18,2},{3,19},{19,3},{4,20},{20... | collective-permute-start | bytes 1572872 | tf_op jit(solution)/shard_map/ppermute | solution.py:434

commit v3 on v2

v3 whole, which is shorter than its diff:
```python
import functools

import jax
import jax.numpy as jnp
from jax import lax
from jax.experimental import pallas as pl
from jax.experimental.pallas import tpu as pltpu
from jax.sharding import PartitionSpec as P


WIDE = 4
SEG = 16
BF = jnp.bfloat16
F32 = jnp.float32


def swap_pairs(size):
    return [(i, i ^ 1) for i in range(size) if i ^ 1 < size]


def shifted_pairs(size):
    up = [(i, i + 1) for i in range(1, size - 1, 2)]
    return up + [(j, i) for i, j in up]


def transposer():
    row = lax.broadcasted_iota(jnp.int32, (256, 256), 0)
    col = lax.broadcasted_iota(jnp.int32, (256, 256), 1)
    hit = ((row >> 4) == (col & 15)) & ((row & 15) == (col >> 4))
    return jnp.where(hit, 1.0, 0.0).astype(BF)


def lane_mask(test):
    lane = lax.broadcasted_iota(jnp.int32, (16, 128), 1)
    return jnp.where(test(lane), 1.0, 0.0).astype(BF)


def swap_rows(turn, blocks):
    wide = jnp.concatenate(blocks, 1) if len(blocks) > 1 else blocks[0]
    turned = jnp.dot(turn, wide, preferred_element_type=F32).astype(BF)
    return [turned[:, k * 128 : (k + 1) * 128].reshape(16, 16, 128) for k in range(len(blocks))]


def fill_table(flip_x, w_ref, b_ref, t_ref):
    zero = jnp.zeros((16, 16), BF)
    flipped = lax.axis_index("gx") == 1 if flip_x else None
    row = lax.broadcasted_iota(jnp.int32, (16, 16), 0)
    col = lax.broadcasted_iota(jnp.int32, (16, 16), 1)
    for layer in range(w_ref.shape[0]):
        for dz in range(3):
            for xo in range(2):
                for yo in range(2):
                    pieces = []
                    for xi in range(4):
                        for yi in range(4):
                            dx, dy = xi - xo, yi - yo
                            if 0 <= dx < 3 and 0 <= dy < 3:
                                at = jnp.where(flipped, 2 - dx, dx) if flip_x else dx
                                pieces.append(w_ref[layer, at, dy, dz])
                            else:
                                pieces.append(zero)
                    at_row = ((dz * 2 + xo) * 2 + yo) * 16
                    t_ref[layer, at_row : at_row + 16] = jnp.concatenate(pieces, 1)
        spread = jnp.broadcast_to(b_ref[layer : layer + 1, :].astype(F32), (16, 16))
        column = jnp.sum(jnp.where(row == col, spread, 0.0), axis=1, keepdims=True)
        t_ref[layer, 192:208] = jnp.broadcast_to(column, (16, 256)).astype(BF)


def pack_kernel(flip_x, x_hbm, w_hbm, b_hbm, tile_ref, z_ref, a_ref, b_ref, t_ref, x_ref, w_ref, bias_ref, sems):
    depth, rows = tile_ref.shape[0], tile_ref.shape[1]
    section = lax.axis_index("segment")
    chans = x_ref.shape[0]
    small = [
        pltpu.make_async_copy(w_hbm, w_ref, sems.at[chans]),
        pltpu.make_async_copy(b_hbm, bias_ref, sems.at[chans + 1]),
    ]
    copies = [pltpu.make_async_copy(x_hbm.at[section, c], x_ref.at[c], sems.at[c]) for c in range(chans)]
    for copy in small + copies:
        copy.start()
    right = lax.axis_index("gz") == 0
    even = lax.rem(lax.axis_index("gy"), 2) == 0
    turned_by = jnp.where(right, WIDE, 0)
    turn = transposer()
    masks = [lane_mask(lambda lane: (((lane + turned_by) & 127) >> 2) == y) for y in range(rows)]
    first = jnp.where(even, rows - WIDE, 0)
    second = jnp.where(even, 0, rows - WIDE)
    for copy in small:
        copy.wait()
    fill_table(flip_x, w_ref, bias_ref, t_ref)
    for copy in copies:
        copy.wait()
    for x in range(depth):
        tiles = []
        for y0 in range(0, rows, 32):
            starts = range(y0, min(y0 + 32, rows), 16)
            for at, block in zip(starts, swap_rows(turn, [x_ref[:, x, k : k + 16, :].reshape(256, 128) for k in starts])):
                tile_ref[x, at : at + 16] = block
                tiles += [block[k] for k in range(16)]
        parts = [jnp.zeros((16, 128), BF) for _ in range(4)]
        for y, tile in enumerate(tiles):
            moved = pltpu.roll(tile, 4 * y, 1) if y else tile
            parts[y % 4] = parts[y % 4] + moved * masks[y]
        total = (parts[0] + parts[1]) + (parts[2] + parts[3])
        z_ref[x] = pltpu.roll(total, turned_by, 1)
        a_ref[x] = tile_ref[x, pl.ds(first, WIDE)]
        b_ref[x] = tile_ref[x, pl.ds(second, WIDE)]


def layer_kernel(two_sided, counts, plan, n_raw, n_edge, n_held, half_ids, *refs):
    fills, steps, _ = plan
    raws, refs = refs[:n_raw], refs[n_raw:]
    halos, refs = refs[:n_edge], refs[n_edge:]
    begins = n_held == 0
    (one_ref, two_ref), refs = refs[:2], refs[2:]
    held, refs = refs[:n_held], refs[n_held:]
    levels, strips, refs = refs[:4], refs[4:8], refs[8:]
    if begins:
        mine_ref, other_ref = one_ref, two_ref
        (t_ref, bias_ref), refs = refs[:2], refs[2:]
    else:
        t_ref, bias_ref = one_ref, two_ref
    halves, refs = refs[: len(half_ids)], refs[len(half_ids) :]
    sem = refs[-1]
    rows = levels[0].shape[1] - 2 - 2 * WIDE
    depth = plan[2]
    ext_rows = rows + 2 * WIDE
    per = strips[0].shape[1] - 2
    segments = 128 // SEG
    section = lax.axis_index("segment")
    gx, gy = lax.axis_index("gx"), lax.axis_index("gy")
    right = lax.axis_index("gz") == 0
    even = lax.rem(gy, 2) == 0
    top_ok = jnp.where(gy == 0, 0.0, 1.0).astype(F32)
    low_ok = jnp.where(gy == counts["gy"] - 1, 0.0, 1.0).astype(F32)
    prev_at = jnp.where(even, WIDE + 1, 0)
    next_at = jnp.where(even, 0, WIDE + 1)
    zero_tile = jnp.zeros((16, 128), BF)
    own_at = WIDE if two_sided else 0

    def flip(i, size):
        return i if two_sided else jnp.where(gx == 1, size - 1 - i, i)

    if begins:
        for v, s in zip(levels, strips):
            for x in (0, 1):
                v[x] = jnp.zeros(v.shape[1:], BF)
                s[x] = jnp.zeros(s.shape[1:], BF)
        for x in range(2, levels[0].shape[0]):
            levels[0][x, 0] = zero_tile
            levels[0][x, ext_rows + 1] = zero_tile
            levels[2][x, 2] = zero_tile
            levels[2][x, ext_rows - 1] = zero_tile

    ahead = jnp.where(right, 3 * WIDE, 0)
    own_masks = [
        lane_mask(
            lambda lane: ((((lane + ahead) & 127) >> 4) == j) & (((lane + ahead) & 15) < 3 * WIDE)
        )
        for j in range(segments)
    ]
    halo_masks = [lane_mask(lambda lane: ((lane >> 4) == j) & ((lane & 15) < WIDE)) for j in range(segments)]
    own_turn = jnp.where(right, 3 * WIDE, WIDE)
    halo_turn = jnp.where(right, 3 * WIDE, 0)
    va, sa = levels[0], strips[0]

    for p, source, place, edge_place in fills:
        q = p + 2
        if place is not None:
            va[q, 1 + WIDE : 1 + WIDE + rows] = raws[source][flip(place, depth)]
        if edge_place is None:
            continue
        h = halos[source]
        i = flip(edge_place, h.shape[0])
        va[q, 1 : 1 + WIDE] = h[i, pl.ds(prev_at, WIDE)]
        va[q, 1 + WIDE + rows : 1 + 2 * WIDE + rows] = h[i, pl.ds(next_at, WIDE)]
        edge_prev = h[i, prev_at + WIDE]
        edge_own = h[i, 2 * WIDE + 2]
        edge_next = h[i, next_at + WIDE]
        for yo in range(per):
            own_sum, halo_sum = zero_tile, zero_tile
            for j in range(segments):
                r = per * j + yo
                if r >= ext_rows:
                    continue
                row = va[q, 1 + r]
                own_sum = own_sum + (pltpu.roll(row, SEG * j, 1) if j else row) * own_masks[j]
                if r < WIDE:
                    edge, lane = edge_prev, WIDE * (rows - WIDE + r)
                elif r < WIDE + rows:
                    edge, lane = edge_own, WIDE * (r - WIDE)
                else:
                    edge, lane = edge_next, WIDE * (r - WIDE - rows)
                by = (SEG * j - lane) % 128
                halo_sum = halo_sum + (pltpu.roll(edge, by, 1) if by else edge) * halo_masks[j]
            sa[q, 1 + yo] = pltpu.roll(own_sum, own_turn, 1) + pltpu.roll(halo_sum, halo_turn, 1)
        sa[q, 0] = pltpu.roll(sa[q, per], SEG, 1)
        sa[q, per + 1] = pltpu.roll(sa[q, 1], 128 - SEG, 1)

    if begins:
        for layer in range(2):
            t_ref[2 * section + layer] = mine_ref[layer]
            t_ref[2 * (1 - section) + layer] = other_ref[layer]
        for layer in range(4):
            one = t_ref[layer, 192:208, :128].astype(F32)
            for k in range(4):
                bias_ref[layer, 16 * k : 16 * (k + 1)] = one

    wide_lane = lax.broadcasted_iota(jnp.int32, (64, 128), 1)
    not_first = jnp.where(wide_lane == 0, 0.0, 1.0)
    not_last = jnp.where(wide_lane == 127, 0.0, 1.0)
    strip_lane = lax.broadcasted_iota(jnp.int32, (16, 128), 1) >> 4

    def strip_ok(yo):
        r = strip_lane * per + yo
        return jnp.where(r < WIDE, top_ok, jnp.where(r >= WIDE + rows, low_ok, 1.0))

    def group(layer, at, part=None):
        src, ssrc = levels[layer], strips[layer]
        last = layer == 3
        dst, sdst = (levels[0], strips[0]) if last else (levels[layer + 1], strips[layer + 1])
        r0, row_groups = ((0, ext_rows // 2), (2, ext_rows // 2 - 2), (2, ext_rows // 2 - 2), (WIDE, rows // 2))[layer]
        margin = WIDE + 2 * (layer + 1)
        inner = [margin <= r0 + 2 * k < ext_rows - margin for k in range(row_groups)]
        items = [(src, r0 + 2 * k, False) for k in range(row_groups) if part is None or inner[k] == (part == 0)]
        if part != 0:
            items += [(ssrc, 2 * k, True) for k in range(per // 2)]
        half = len(items) // 2
        order = [[items[k], items[half + k]] for k in range(half)] + [[t] for t in items[2 * half :]]
        for pair in order:
            columns = [
                jnp.concatenate([ref[at + 1 + xi, r : r + 4].reshape(64, 128) for xi in range(4)], 0)
                for ref, r, _ in pair
            ]
            wide = jnp.concatenate(columns, 1) if len(columns) > 1 else columns[0]
            got = jnp.dot(t_ref[layer, :192], wide, preferred_element_type=F32)
            for k, (_, r, strip) in enumerate(pair):
                part = got[:, 128 * k : 128 * (k + 1)]
                a = part[64:128] + pltpu.roll(part[:64], 1, 1) * not_first
                a = a + pltpu.roll(part[128:], 127, 1) * not_last
                a = a + bias_ref[layer]
                a = jnp.maximum(a, 0.2 * a)
                for xo in range(2):
                    place = at + xo
                    if isinstance(place, int) and place < 0:
                        continue
                    for yo in range(2):
                        one = a[(2 * xo + yo) * 16 : (2 * xo + yo + 1) * 16]
                        if not last:
                            if strip:
                                one = one * strip_ok(r + yo)
                            elif r + yo < WIDE:
                                one = one * top_ok
                            elif r + yo >= WIDE + rows:
                                one = one * low_ok
                            if two_sided:
                                outside = ((place < WIDE) & (gx == 0)) | (
                                    (place >= WIDE + depth) & (gx == counts["gx"] - 1)
                                )
                                one = one * jnp.where(outside, 0.0, 1.0)
                        one = one.astype(BF)
                        if strip:
                            sdst[place + 2, r + yo + 1] = one
                            if r + yo == 0:
                                sdst[place + 2, per + 1] = pltpu.roll(one, 128 - SEG, 1)
                            if r + yo == per - 1:
                                sdst[place + 2, 0] = pltpu.roll(one, SEG, 1)
                        else:
                            dst[place + 2, r + yo + 1] = one

    def emit(part, half):
        turn = transposer()
        edge_turn = jnp.where(right, 0, 2 * WIDE)
        edge_ahead = jnp.where(right, WIDE, 0)
        edge_mask = lane_mask(lambda lane: ((lane + edge_ahead) & 127) < WIDE)
        inner_mask = lane_mask(lambda lane: ((lane + edge_ahead) & 127) >= WIDE)
        v, s = (levels[2], strips[2]) if part == 0 else (levels[0], strips[0])
        out_ref = halves[half_ids.index(half)]
        role = jnp.where(section == part, 0, 1)
        size = out_ref.shape[2]
        for i in range(size):
            p = own_at + half * size + i
            to = flip(i, size)
            starts = list(range(0, rows, 16))
            for k in range(0, len(starts), 2):
                some = starts[k : k + 2]
                blocks = []
                for y0 in some:
                    tiles = []
                    for y in range(y0, y0 + 16):
                        r = y + WIDE
                        j, yo = r // per, r % per
                        by = (128 - 3 * WIDE - SEG * j) % 128
                        edge = pltpu.roll(s[p + 2, yo + 1], by + edge_turn, 1)
                        tiles.append(v[p + 2, r + 1] * inner_mask + edge * edge_mask)
                    blocks.append(jnp.concatenate(tiles, 0))
                for y0, block in zip(some, swap_rows(turn, blocks)):
                    out_ref[role, :, to, y0 : y0 + 16] = block

    def keep(finish):
        source = halves[0] if begins else held[8]
        size = source.shape[2]
        start = flip(0, 2) * size
        copy = pltpu.make_async_copy(source.at[0], refs[0].at[section, :, pl.ds(start, size)], sem)
        (copy.wait if finish else copy.start)()

    for step in steps:
        if step[0] == "emit":
            emit(*step[1:])
        elif step[0] == "keep":
            keep(step[1])
        elif step[0] == "loop":
            _, layer, x0, n = step

            def body(g, carry):
                group(layer, x0 + 2 * g)
                return carry

            lax.fori_loop(0, n, body, 0)
        else:
            group(*step[1:])


def place_kernel(two_sided, moves, *refs):
    sources, out_ref, sems = refs[1:-2], refs[-2], refs[-1]
    section = lax.axis_index("segment")
    flipped = False if two_sided else lax.axis_index("gx") == 1
    copies = []
    for k, (own, half) in enumerate(moves):
        source = sources[k].at[0] if own else sources[k]
        size = source.shape[1]
        start = half * size if two_sided else jnp.where(flipped, 1 - half, half) * size
        place = out_ref.at[section if own else 1 - section, :, pl.ds(start, size)]
        copies.append(pltpu.make_async_copy(source, place, sems.at[k]))
    for copy in copies:
        copy.start()
    for copy in copies:
        copy.wait()


VMEM = pl.BlockSpec(memory_space=pltpu.VMEM)
ANY = pl.BlockSpec(memory_space=pl.ANY)


def shards(counts, features, weights, biases):
    gx, gy, gz = (counts[a] for a in ("gx", "gy", "gz"))
    two_sided = gx != 2
    micro, chans, depth, rows, lanes = features.shape
    edge = jax.ShapeDtypeStruct((depth, WIDE, chans, lanes), BF)
    hbm = pl.BlockSpec(memory_space=pltpu.HBM)
    in_hbm = lambda v: pltpu.with_memory_space_constraint(v, pltpu.HBM)
    tiles, edge_z, edge_a, edge_b, table = pl.pallas_call(
        functools.partial(pack_kernel, not two_sided),
        out_shape=(
            jax.ShapeDtypeStruct((depth, rows, chans, lanes), BF),
            jax.ShapeDtypeStruct((depth, chans, lanes), BF),
            edge,
            edge,
            jax.ShapeDtypeStruct((2, 208, 256), BF),
        ),
        in_specs=[hbm] * 3,
        out_specs=(VMEM,) * 5,
        scratch_shapes=[
            pltpu.VMEM((chans, depth, rows, lanes), BF),
            pltpu.VMEM((2, 3, 3, 3, chans, chans), BF),
            pltpu.VMEM((2, chans), BF),
            pltpu.SemaphoreType.DMA((chans + 2,)),
        ],
        name="pack",
        compiler_params=pltpu.CompilerParams(vmem_limit_bytes=4 << 20),
        cost_estimate=pl.CostEstimate(flops=4_000_000, bytes_accessed=1_000_000, transcendentals=0),
    )(in_hbm(features), in_hbm(jnp.transpose(weights[0], (0, 3, 4, 5, 1, 2))), in_hbm(biases[0]))

    def along_x(low, high):
        if not two_sided:
            return [lax.ppermute(low, "gx", swap_pairs(2))]
        up = [(i, i + 1) for i in range(gx - 1)]
        return [lax.ppermute(high, "gx", up), lax.ppermute(low, "gx", [(j, i) for i, j in up])]

    raws = along_x(tiles, tiles)
    from_z = lax.ppermute(edge_z, "gz", swap_pairs(gz))
    at_z = from_z[:, None]
    from_b = lax.ppermute(
        jnp.concatenate([edge_b, at_z], 1), "gy", shifted_pairs(gy)
    )
    from_a = lax.ppermute(jnp.concatenate([edge_a, at_z], 1), "gy", swap_pairs(gy))
    halo = jnp.concatenate([from_a, from_b, at_z], 1)
    half = depth // 2
    if two_sided:
        halos = along_x(halo, halo)
    else:
        start = jnp.where(lax.axis_index("gx") == 0, half, 0)
        near_halo = along_x(lax.dynamic_slice_in_dim(halo, start, half, 0), None)
        far_halo = along_x(lax.dynamic_slice_in_dim(halo, half - start, half, 0), None)

    other = lax.ppermute(table, "segment", swap_pairs(2))
    ext = depth + (2 * WIDE if two_sided else WIDE)
    ext_rows = rows + 2 * WIDE
    per = -(-ext_rows * SEG // 128)
    per += per % 2
    state = [jax.ShapeDtypeStruct((ext + 2, ext_rows + 2, chans, lanes), BF)] * 4
    state += [jax.ShapeDtypeStruct((ext + 2, per + 2, chans, lanes), BF)] * 4
    half_shape = jax.ShapeDtypeStruct((2, chans, half, rows, lanes), BF)
    keep_shape = jax.ShapeDtypeStruct((micro, chans, depth, rows, lanes), BF)

    def stage(plan, blocks, edges, pair, before=(), aliases=(), half_ids=(), keeps=False):
        n = len(blocks)
        start = n + len(edges) + 2
        shapes = list(state)
        if not before:
            shapes += [jax.ShapeDtypeStruct((4, 208, 256), BF), jax.ShapeDtypeStruct((4, 64, 128), F32)]
        shapes += [half_shape] * len(half_ids)
        return pl.pallas_call(
            functools.partial(layer_kernel, two_sided, counts, (*plan, depth), n, len(edges), len(before), half_ids),
            out_shape=shapes + ([keep_shape] if keeps else []),
            in_specs=[VMEM] * (start + len(before)),
            out_specs=[VMEM] * len(shapes) + ([ANY] if keeps else []),
            scratch_shapes=[pltpu.SemaphoreType.DMA],
            input_output_aliases={start + i: o for i, o in aliases},
            compiler_params=pltpu.CompilerParams(vmem_limit_bytes=24 << 20),
            cost_estimate=pl.CostEstimate(flops=2_000_000_000, bytes_accessed=4_000_000, transcendentals=0),
        )(*blocks, *edges, *pair, *before)

    def place(whole, sources, moves):
        return pl.pallas_call(
            functools.partial(place_kernel, two_sided, moves),
            out_shape=keep_shape,
            in_specs=[ANY] + [VMEM] * len(sources),
            out_specs=ANY,
            scratch_shapes=[pltpu.SemaphoreType.DMA((len(sources),))],
            input_output_aliases={0: 0},
            name="place",
            compiler_params=pltpu.CompilerParams(vmem_limit_bytes=2 << 20),
            cost_estimate=pl.CostEstimate(flops=0, bytes_accessed=500_000, transcendentals=0),
        )(whole, *sources)

    def chain(k, part=None):
        return [("one", layer, 2 * k - 1 - layer, part) for layer in range(4) if 2 * k - layer >= 0]

    if two_sided:
        fills = [(p, 1, depth - WIDE + p, depth - WIDE + p) for p in range(WIDE)]
        fills += [(WIDE + p, 0, p, p) for p in range(depth)]
        fills += [(WIDE + depth + p, 2, p, p) for p in range(WIDE)]
        steps = []
        for layer in range(4):
            steps.append(("loop", layer, layer + 1, (ext - 2 * layer - 2) // 2))
            if layer % 2:
                steps += [("emit", layer // 2, 0), ("emit", layer // 2, 1)]
        steps += [("keep", False), ("keep", True)]
        *_, first, second, whole = stage(
            (fills, steps), [tiles, *raws], [halo, *halos], (table, other), half_ids=(0, 1), keeps=True
        )
    else:
        same = [(k, k) for k in range(8)]
        fills = [(p, 0, p, None) for p in range(depth)]
        steps = chain(0, 0) + chain(1, 0)
        *state_now, t, bias = stage((fills, steps), [tiles], [], (table, other))
        fills = [(p, 0, None, p) for p in range(depth)]
        steps = chain(0, 1) + chain(1, 1) + [("emit", 0, 0)]
        *state_now, first = stage((fills, steps), [], [halo], (t, bias), state_now, same, (0,))
        fills = [(depth + p, 0, p, p) for p in range(half)]
        steps = chain(2)[:2] + [("emit", 0, 1)] + chain(2)[2:] + [("emit", 1, 0)]
        *state_now, first, second = stage(
            (fills, steps), raws, near_halo, (t, bias), [*state_now, first], same + [(8, 8)], (0, 1)
        )
        fills = [(depth + p, 0, p, p - half) for p in range(half, WIDE)]
        steps = [("keep", False)] + chain(3) + [("emit", 1, 1), ("keep", True)]
        *_, second, whole = stage(
            (fills, steps), raws, far_halo, (t, bias), [*state_now, first, second], same + [(9, 8)], (1,), True
        )

    got_first = lax.ppermute(first[1], "segment", swap_pairs(2))
    got_second = lax.ppermute(second[1], "segment", swap_pairs(2))
    whole = place(whole, [second, got_first], ((True, 1), (False, 0)))
    return place(whole, [got_second], ((False, 1),))[None]


def solution(mesh):
    placed = (
        P(None, None, "gx", "gy", "gz"),
        P("segment", None, None, None, None, None, None),
        P("segment", None, None),
    )

    def step(*args):
        return shards(dict(mesh.shape), *args)

    return jax.shard_map(
        step,
        mesh=mesh,
        in_specs=placed,
        out_specs=P("segment", None, None, "gx", "gy", "gz"),
        check_vma=False,
    )
```

time: 35.2 us -> 37.2 us (1.057)
  the two profiles are of different devices: /device:TPU:0 before, /device:TPU:9 now
where the time goes in v3:
time: 37.2 us; the launch traced here: 37.1 us
  Pallas kernels  13 us (35%)
  starting transfers between devices  12.7 us (34%)
  waiting for transfers between devices  11.2 us (30%)
    pallas_call x4, Pallas kernels, stage(): pl.pallas_call(functools.partial(layer_kernel, two_sided, counts, (*plan,...  9.52 us
    ppermute x3, waiting for transfers between devices, along_x(): return [lax.ppermute(low, 'gx', swap_pairs(2))]  9.17 us
    ppermute x1, starting transfers between devices, shards(): lax.ppermute(jnp.concatenate([edge_b, at_z], 1), 'gy', shifted_pairs(gy))  4.48 us
    ppermute x3, starting transfers between devices, along_x(): return [lax.ppermute(low, 'gx', swap_pairs(2))]  2.74 us
    ppermute x1, starting transfers between devices, shards(): other = lax.ppermute(table, 'segment', swap_pairs(2))  2.45 us
    pallas_call x1, Pallas kernels, shards(): pl.pallas_call(functools.partial(pack_kernel, not two_sided), out_shape=(...  1.93 us
    ppermute x1, starting transfers between devices, shards(): got_first = lax.ppermute(first[1], 'segment', swap_pairs(2))  1.55 us
    pallas_call x2, Pallas kernels, place(): pl.pallas_call(functools.partial(place_kernel, two_sided, moves), out_sha...  1.53 us
  transfers between devices with their start and end apart: 9, of which 3 were waited for; matrix products, arithmetic and copies ran while one was open for 0% of the time, Pallas kernels for 28%

profile of v3, /device:TPU:9, one launch (start us, length us, event | category | flops | bytes accessed | tf_op | source)
XLA Modules:
  0.0 37.1 jit_solution(11917867680637321802)
XLA Ops:
  0.0 1.9 %pack.1 = (bf16[4,32,16,128]{3,2,1,0:T(8,128)(2,1)S(1)}, bf16[4,16,128]{2,1,0:T(8,128)(2,1)S(1)}, bf16[4,4,16,128]{3,2,1,0:T(8,128)(2,1)S(1)}, bf16[4,4,16,128]{...) custom-call(bf16[2,16,4,32,128]{4,3,2,1,0:T(8,128)(2,1)} %x_hbm.1, bf16[2,3,3,3,16,16]{5,4,3,2,1,0:T(8,128)(2,1)} %bitcast.10, ...), custom_call_target="tpu_custom_call" | custom-call | flops 4000000 | bytes 1000000 | tf_op jit(solution)/shard_map/pack/pallas_call | solution.py:351
  1.9 1.3 %collective-permute-start.1 = (bf16[4,16,128]{2,1,0:T(8,128)(2,1)S(1)}, bf16[4,16,128]{2,1,0:T(8,128)(2,1)S(1)}, u32[]{:S(2)}, u32[]{:S(2)}) collective-permute-start(bf16[4,16,128]{2,1,0:T(8,128)(2,1)S(1)} %get-tuple-element.43), channel_id=1, source_target_pairs={{0,1},{1,0},{2,3},{3,2},{4,5},{5,4},{6,7},{7,6},{8,9},{9,8},{10,11... | collective-permute-start | bytes 49160 | tf_op jit(solution)/shard_map/ppermute | solution.py:380
  3.2 1.3 %collective-permute-done.1 = bf16[4,16,128]{2,1,0:T(8,128)(2,1)S(1)} collective-permute-done((bf16[4,16,128]{2,1,0:T(8,128)(2,1)S(1)}, bf16[4,16,128]{2,1,0:T(8,128)(2,1)S(1)}, u32[]{:S(2)}, u32[]{:S(2)}) %collective-permute-start.1) | collective-permute-done | bytes 16416 | tf_op jit(solution)/shard_map/ppermute | solution.py:380
  4.6 0.1 collective-permute-start.2
  4.7 4.5 %collective-permute-start.3 = (bf16[4,5,16,128]{3,2,1,0:T(8,128)(2,1)S(1)}, bf16[4,5,16,128]{3,2,1,0:T(8,128)(2,1)S(1)}, u32[]{:S(2)}, u32[]{:S(2)}) collective-permute-start(bf16[4,5,16,128]{3,2,1,0:T(8,128)(2,1)S(1)} %get-tuple-element.80), channel_id=1, source_target_pairs={{2,4},{4,2},{3,5},{5,3},{10,12},{12,10},{11,13},{13,11},{18,20},{2... | collective-permute-start | bytes 245768 | tf_op jit(solution)/shard_map/ppermute | solution.py:382
  9.2 2.5 %collective-permute-start.5 = (bf16[2,208,256]{2,1,0:T(8,128)(2,1)S(1)}, bf16[2,208,256]{2,1,0:T(8,128)(2,1)S(1)}, u32[]{:S(2)}, u32[]{:S(2)}) collective-permute-start(bf16[2,208,256]{2,1,0:T(8,128)(2,1)S(1)} %get-tuple-element.45.refs_1_), channel_id=1, source_target_pairs={{0,16},{16,0},{1,17},{17,1},{2,18},{18,2},{3,19},{19,3},{4,20},{20... | collective-permute-start | bytes 638984 | tf_op jit(solution)/shard_map/ppermute | solution.py:395
  11.6 1.2 %collective-permute-start = (bf16[4,32,16,128]{3,2,1,0:T(8,128)(2,1)S(1)}, bf16[4,32,16,128]{3,2,1,0:T(8,128)(2,1)S(1)}, u32[]{:S(2)}, u32[]{:S(2)}) collective-permute-start(bf16[4,32,16,128]{3,2,1,0:T(8,128)(2,1)S(1)} %get-tuple-element.41.refs_0_), channel_id=1, source_target_pairs={{0,8},{8,0},{1,9},{9,1},{2,10},{10,2},{3,11},{11,3},{4,12},{12,4},... | collective-permute-start | bytes 1572872 | tf_op jit(solution)/shard_map/ppermute | solution.py:375
  12.8 0.0 collective-permute-done.2
  12.8 0.0 collective-permute-done.3
  12.9 0.3 collective-permute-start.6
  13.2 1.2 %collective-permute-start.4 = (bf16[2,11,16,128]{3,2,1,0:T(8,128)(2,1)S(1)}, bf16[2,11,16,128]{3,2,1,0:T(8,128)(2,1)S(1)}, u32[]{:S(2)}, u32[]{:S(2)}) collective-permute-start(bf16[2,11,16,128]{3,2,1,0:T(8,128)(2,1)S(1)} %get-tuple-element.78), channel_id=1, source_target_pairs={{0,8},{8,0},{1,9},{9,1},{2,10},{10,2},{3,11},{11,3},{4,12},{12,4},... | collective-permute-start | bytes 270344 | tf_op jit(solution)/shard_map/ppermute | solution.py:375
  14.4 0.0 collective-permute-done.5.refs_2_
  14.4 1.5 %shard_map.37 = (bf16[10,42,16,128]{3,2,1,0:T(8,128)(2,1)S(1)}, bf16[10,42,16,128]{3,2,1,0:T(8,128)(2,1)S(1)}, bf16[10,42,16,128]{3,2,1,0:T(8,128)(2,1)S(1)}, bf...) custom-call(bf16[4,32,16,128]{3,2,1,0:T(8,128)(2,1)S(1)} %get-tuple-, ...), custom_call_target="tpu_custom_call" | custom-call | flops 2000000000 | bytes 4000000 | tf_op jit(solution)/shard_map/pallas_call | solution.py:412
  15.9 1.9 %shard_map.38 = (bf16[10,42,16,128]{3,2,1,0:T(8,128)(2,1)S(1)}, bf16[10,42,16,128]{3,2,1,0:T(8,128)(2,1)S(1)}, bf16[10,42,16,128]{3,2,1,0:T(8,128)(2,1)S(1)}, bf...) custom-call(bf16[4,11,16,128]{3,2,1,0:T(8,128)(2,1)S(1)} %pad_maximu, ...), custom_call_target="tpu_custom_call", output_to_operand_aliasing={{0}: (3, {}), {1}: (4, {}), {2}: (5, {}), {3}: (6, {}), {4}... | custom-call | flops 2000000000 | bytes 4000000 | tf_op jit(solution)/shard_map/pallas_call | solution.py:412
  17.8 9.2 %collective-permute-done.6.refs_1_ = bf16[2,11,16,128]{3,2,1,0:T(8,128)(2,1)S(1)} collective-permute-done((bf16[2,11,16,128]{3,2,1,0:T(8,128)(2,1)S(1)}, bf16[2,11,16,128]{3,2,1,0:T(8,128)(2,1)S(1)}, u32[]{:S(2)}, u32[]{:S(2)}) %collective-permute-start.6) | collective-permute-done | bytes 90144 | tf_op jit(solution)/shard_map/ppermute | solution.py:375
  27.0 0.0 collective-permute-done.refs_0_
  27.0 3.1 %shard_map.39 = (bf16[10,42,16,128]{3,2,1,0:T(8,128)(2,1)S(1)}, bf16[10,42,16,128]{3,2,1,0:T(8,128)(2,1)S(1)}, bf16[10,42,16,128]{3,2,1,0:T(8,128)(2,1)S(1)}, bf...) custom-call(bf16[4,32,16,128]{3,2,1,0:T(8,128)(2,1)S(1)} %collective, ...), custom_call_target="tpu_custom_call", output_to_operand_aliasing={{0}: (4, {}), {1}: (5, {}), {2}: (6, {}), {3}: (7, {}), {4}... | custom-call | flops 2000000000 | bytes 4000000 | tf_op jit(solution)/shard_map/pallas_call | solution.py:412
  30.1 1.5 %collective-permute-start.7 = (bf16[16,2,32,128]{3,2,1,0:T(8,128)(2,1)S(1)}, bf16[16,2,32,128]{3,2,1,0:T(8,128)(2,1)S(1)}, u32[]{:S(2)}, u32[]{:S(2)}) collective-permute-start(bf16[16,2,32,128]{3,2,1,0:T(8,128)(2,1)S(1)} %slice_bitcast_fusion.1), channel_id=1, source_target_pairs={{0,16},{16,0},{1,17},{17,1},{2,18},{18,2},{3,19},{19,3},{4,20},{20... | collective-permute-start | bytes 786440 | tf_op jit(solution)/shard_map/ppermute | solution.py:471
  31.6 0.0 collective-permute-done.4.refs_1_
  31.6 3.1 %shard_map.40 = (bf16[10,42,16,128]{3,2,1,0:T(8,128)(2,1)S(1)}, bf16[10,42,16,128]{3,2,1,0:T(8,128)(2,1)S(1)}, bf16[10,42,16,128]{3,2,1,0:T(8,128)(2,1)S(1)}, bf...) custom-call(bf16[4,32,16,128]{3,2,1,0:T(8,128)(2,1)S(1)} %collective, ...), custom_call_target="tpu_custom_call", output_to_operand_aliasing={{0}: (4, {}), {1}: (5, {}), {2}: (6, {}), {3}: (7, {}), {4}... | custom-call | flops 2000000000 | bytes 4000000 | tf_op jit(solution)/shard_map/pallas_call | solution.py:412
  34.8 0.1 collective-permute-start.8
  34.9 0.0 collective-permute-done.7.refs_2_
  34.9 0.8 %place.2.refs_0_ = bf16[2,16,4,32,128]{4,3,2,1,0:T(8,128)(2,1)} custom-call(bf16[2,16,4,32,128]{4,3,2,1,0:T(8,128)(2,1)} %get-tuple-element.75.refs_0_, bf16[2,16,2,32,128]{4,3,2,1,0:T(8,128)(2,1)S(1)} %get-tuple-element.76.refs_1_, bf16[16,2,32,128]{3,2,1,0:T(8,128)(2,1)S(1)} %collective-permute-done.7.refs_2_), custom_call_target="tpu_custom_call", output_to_operand_aliasing={{}: (0, {})} | custom-call | bytes 500000 | tf_op jit(solution)/shard_map/place/pallas_call | solution.py:424
  35.7 0.7 %collective-permute-done.8.refs_1_ = bf16[16,2,32,128]{3,2,1,0:T(8,128)(2,1)S(1)} collective-permute-done((bf16[16,2,32,128]{3,2,1,0:T(8,128)(2,1)S(1)}, bf16[16,2,32,128]{3,2,1,0:T(8,128)(2,1)S(1)}, u32[]{:S(2)}, u32[]{:S(2)}) %collective-permute-start.8) | collective-permute-done | bytes 262176 | tf_op jit(solution)/shard_map/ppermute | solution.py:472
  36.4 0.7 %place.3 = bf16[2,16,4,32,128]{4,3,2,1,0:T(8,128)(2,1)} custom-call(bf16[2,16,4,32,128]{4,3,2,1,0:T(8,128)(2,1)} %place.2.refs_0_, bf16[16,2,32,128]{3,2,1,0:T(8,128)(2,1)S(1)} %collective-permute-done.8.refs_1_), custom_call_target="tpu_custom_call", output_to_operand_aliasing={{}: (0, {})} | custom-call | bytes 500000 | tf_op jit(solution)/shard_map/place/pallas_call | solution.py:424
  (5 shorter events, 0.1 us)
Async XLA Ops:
  1.9 2.7 %collective-permute-start.1 = (bf16[4,16,128]{2,1,0:T(8,128)(2,1)S(1)}, bf16[4,16,128]{2,1,0:T(8,128)(2,1)S(1)}, u32[]{:S(2)}, u32[]{:S(2)}) collective-permute-start(bf16[4,16,128]{2,1,0:T(8,128)(2,1)S(1)} %get-tuple-element.43), channel_id=1, source_target_pairs={{0,1},{1,0},{2,3},{3,2},{4,5},{5,4},{6,7},{7,6},{8,9},{9,8},{10,11... | collective-permute-start | bytes 49160 | tf_op jit(solution)/shard_map/ppermute | solution.py:380
  4.6 8.2 %collective-permute-start.2 = (bf16[4,5,16,128]{3,2,1,0:T(8,128)(2,1)S(1)}, bf16[4,5,16,128]{3,2,1,0:T(8,128)(2,1)S(1)}, u32[]{:S(2)}, u32[]{:S(2)}) collective-permute-start(bf16[4,5,16,128]{3,2,1,0:T(8,128)(2,1)S(1)} %get-tuple-element.79), channel_id=1, source_target_pairs={{0,2},{2,0},{4,6},{6,4},{1,3},{3,1},{5,7},{7,5},{8,10},{10,8},{12,... | collective-permute-start | bytes 245768 | tf_op jit(solution)/shard_map/ppermute | solution.py:385
  4.7 8.2 %collective-permute-start.3 = (bf16[4,5,16,128]{3,2,1,0:T(8,128)(2,1)S(1)}, bf16[4,5,16,128]{3,2,1,0:T(8,128)(2,1)S(1)}, u32[]{:S(2)}, u32[]{:S(2)}) collective-permute-start(bf16[4,5,16,128]{3,2,1,0:T(8,128)(2,1)S(1)} %get-tuple-element.80), channel_id=1, source_target_pairs={{2,4},{4,2},{3,5},{5,3},{10,12},{12,10},{11,13},{13,11},{18,20},{2... | collective-permute-start | bytes 245768 | tf_op jit(solution)/shard_map/ppermute | solution.py:382
  9.2 5.3 %collective-permute-start.5 = (bf16[2,208,256]{2,1,0:T(8,128)(2,1)S(1)}, bf16[2,208,256]{2,1,0:T(8,128)(2,1)S(1)}, u32[]{:S(2)}, u32[]{:S(2)}) collective-permute-start(bf16[2,208,256]{2,1,0:T(8,128)(2,1)S(1)} %get-tuple-element.45.refs_1_), channel_id=1, source_target_pairs={{0,16},{16,0},{1,17},{17,1},{2,18},{18,2},{3,19},{19,3},{4,20},{20... | collective-permute-start | bytes 638984 | tf_op jit(solution)/shard_map/ppermute | solution.py:395
  11.6 15.3 %collective-permute-start = (bf16[4,32,16,128]{3,2,1,0:T(8,128)(2,1)S(1)}, bf16[4,32,16,128]{3,2,1,0:T(8,128)(2,1)S(1)}, u32[]{:S(2)}, u32[]{:S(2)}) collective-permute-start(bf16[4,32,16,128]{3,2,1,0:T(8,128)(2,1)S(1)} %get-tuple-element.41.refs_0_), channel_id=1, source_target_pairs={{0,8},{8,0},{1,9},{9,1},{2,10},{10,2},{3,11},{11,3},{4,12},{12,4},... | collective-permute-start | bytes 1572872 | tf_op jit(solution)/shard_map/ppermute | solution.py:375
  12.9 14.1 %collective-permute-start.6 = (bf16[2,11,16,128]{3,2,1,0:T(8,128)(2,1)S(1)}, bf16[2,11,16,128]{3,2,1,0:T(8,128)(2,1)S(1)}, u32[]{:S(2)}, u32[]{:S(2)}) collective-permute-start(bf16[2,11,16,128]{3,2,1,0:T(8,128)(2,1)S(1)} %get-tuple-element.77), channel_id=1, source_target_pairs={{0,8},{8,0},{1,9},{9,1},{2,10},{10,2},{3,11},{11,3},{4,12},{12,4},... | collective-permute-start | bytes 270344 | tf_op jit(solution)/shard_map/ppermute | solution.py:375
  13.2 18.4 %collective-permute-start.4 = (bf16[2,11,16,128]{3,2,1,0:T(8,128)(2,1)S(1)}, bf16[2,11,16,128]{3,2,1,0:T(8,128)(2,1)S(1)}, u32[]{:S(2)}, u32[]{:S(2)}) collective-permute-start(bf16[2,11,16,128]{3,2,1,0:T(8,128)(2,1)S(1)} %get-tuple-element.78), channel_id=1, source_target_pairs={{0,8},{8,0},{1,9},{9,1},{2,10},{10,2},{3,11},{11,3},{4,12},{12,4},... | collective-permute-start | bytes 270344 | tf_op jit(solution)/shard_map/ppermute | solution.py:375
  30.1 4.8 %collective-permute-start.7 = (bf16[16,2,32,128]{3,2,1,0:T(8,128)(2,1)S(1)}, bf16[16,2,32,128]{3,2,1,0:T(8,128)(2,1)S(1)}, u32[]{:S(2)}, u32[]{:S(2)}) collective-permute-start(bf16[16,2,32,128]{3,2,1,0:T(8,128)(2,1)S(1)} %slice_bitcast_fusion.1), channel_id=1, source_target_pairs={{0,16},{16,0},{1,17},{17,1},{2,18},{18,2},{3,19},{19,3},{4,20},{20... | collective-permute-start | bytes 786440 | tf_op jit(solution)/shard_map/ppermute | solution.py:471
  34.8 1.6 %collective-permute-start.8 = (bf16[16,2,32,128]{3,2,1,0:T(8,128)(2,1)S(1)}, bf16[16,2,32,128]{3,2,1,0:T(8,128)(2,1)S(1)}, u32[]{:S(2)}, u32[]{:S(2)}) collective-permute-start(bf16[16,2,32,128]{3,2,1,0:T(8,128)(2,1)S(1)} %slice_bitcast_fusion), channel_id=1, source_target_pairs={{0,16},{16,0},{1,17},{17,1},{2,18},{18,2},{3,19},{19,3},{4,20},{20... | collective-permute-start | bytes 786440 | tf_op jit(solution)/shard_map/ppermute | solution.py:472
